TPU v7x, 32 devices: a whole 2x2x4 slice. The times are simulated.
32 devices in a mesh: depth: 4 (over z), rows: 8 (over y, x, core).
Axes of the slice: x: 2, y: 2, z: 4, core: 2. Of those that a mesh axis runs over, the one named last changes fastest.
Arguments:
- density: float32 [64, 1024, 2048], P('depth', 'rows'), may hold values from 0.2 to 3
- occupancy: int32 [4, 8, 16], P('depth', 'rows'), may hold values from 0 to 1, as said below
- transfer: float32 [2, 4], replicated, may hold values from -1.5 to 1.5
Outputs:
- image: float32 [4, 1024, 2048], P(None, 'rows', 'depth')
Inputs may be any that keep to these rules, and one draw needn't show every extreme that they name: `occupancy`: each entry is 0 or 1 and flags a block of 16 x 128 x 128 cells as occupied; at most 12 of the blocks of one device's brick are occupied, and some brick has exactly 12.
All inputs are finite; a program needn't handle non-finite values.
Results may differ from a plain program's by a relative error of at most 0.000079.
Values sent between devices are 32-bit elements; how exact they have to be, the bound alone decides.
No kernel may reach another device: no remote copies, remote signals or barrier semaphores. Data moves between devices by JAX's collectives and lax.ppermute only.
A program may use at most 256 MiB of HBM per device.

v0:
```python
import jax
import jax.numpy as jnp
from jax import lax
from jax.sharding import PartitionSpec as P


def extended_2(cells, sides, width):
    for axis, dim in sides:
        count = lax.axis_size(axis)
        ends = count - 1
        head = lax.slice_in_dim(cells, 0, width, axis=dim)
        tail = lax.slice_in_dim(cells, cells.shape[dim] - width, cells.shape[dim], axis=dim)
        cells = jnp.concatenate(
            [
                lax.ppermute(tail, axis, [(i, (i + 1) % count) for i in range(ends)]),
                cells,
                lax.ppermute(head, axis, [((i + 1) % count, i) for i in range(ends)]),
            ],
            axis=dim,
        )
    return cells


def swapped(block, axis, bit):
    count = lax.axis_size(axis)
    route = []
    for low in range(count):
        high = low | 1 << bit
        if high != low and high < count:
            route += [(low, high), (high, low)]
    return lax.ppermute(block, axis, route)


def shade(center, grad_z, grad_y, grad_x, transfer, ray_step):
    inv_norm = 1.0 / jnp.sqrt(grad_x * grad_x + grad_y * grad_y + grad_z * grad_z + 1.0)
    lighting = 0.3 + 0.7 * jnp.abs((0.48 * grad_z + 0.6 * grad_y + 0.64 * grad_x) * inv_norm)
    extinct = center * jax.nn.softplus(transfer[0, 3] * center + transfer[1, 3])
    opacity = 1.0 - jnp.exp(-ray_step * extinct)
    colors = jnp.stack(
        [
            jax.nn.sigmoid(transfer[0, channel] * center + transfer[1, channel])
            for channel in range(3)
        ]
    )
    return (opacity * lighting * colors, opacity)


def voxels(window, transfer, ray_step):
    center = window[1, 1:-1, ..., 1:-1]
    grad_z = (window[2, 1:-1, ..., 1:-1] - window[0, 1:-1, ..., 1:-1]) * 0.5
    grad_y = (window[1, 2:, ..., 1:-1] - window[1, :-2, ..., 1:-1]) * 0.5
    grad_x = (window[1, 1:-1, ..., 2:] - window[1, 1:-1, ..., :-2]) * 0.5
    return shade(center, grad_z, grad_y, grad_x, transfer, ray_step)


def march(padded, transfer, ray_step):
    depth_count = padded.shape[0] - 2
    cell_shape = (padded.shape[1] - 2,) + padded.shape[2:-1] + (padded.shape[-1] - 2,)
    start_state = (jnp.zeros((3,) + cell_shape, jnp.float32), jnp.ones(cell_shape, jnp.float32))

    def advance(state_pair, depth_at):
        color_sum, transmit = state_pair
        window = lax.dynamic_slice_in_dim(padded, depth_at, 3, 0)
        shaded, opacity = voxels(window, transfer, ray_step)
        return ((color_sum + transmit * shaded, transmit * (1.0 - opacity)), None)

    (color_sum, transmit), _ = lax.scan(
        advance, start_state, jnp.arange(depth_count, dtype=jnp.int32)
    )
    return (color_sum, transmit)


def blend_over(front_part, back_part):
    color_sum = front_part[:3] + front_part[3:] * back_part[:3]
    transmit = front_part[3:] * back_part[3:]
    return jnp.concatenate([color_sum, transmit], 0)


def shards(density, occupancy, transfer):
    depth_cells, row_cells, col_cells = density.shape
    block_flags = occupancy.reshape(-1)
    block_count = block_flags.shape[0]
    block_width = col_cells // block_count
    depth_devices = lax.axis_size("depth")
    position = lax.axis_index("depth")
    masked = (
        density.reshape(depth_cells, row_cells, block_count, block_width)
        * block_flags.astype(jnp.float32)[None, None, :, None]
    )
    masked = masked.reshape(depth_cells, row_cells, col_cells)
    extended = extended_2(masked, (("depth", 0), ("rows", 1)), 1)
    ray_step = 2.0 / (depth_cells * depth_devices)
    padded = jnp.pad(extended, ((0, 0), (0, 0), (1, 1)))
    color_sum, transmit = march(padded, transfer, ray_step)
    layers = jnp.concatenate([color_sum, transmit[None]], 0)
    piece_width = col_cells // depth_devices
    levels = depth_devices.bit_length() - 1
    merged = layers.reshape((4, row_cells) + (2,) * levels + (piece_width,))
    for bit_level in range(levels):
        axis_at = 2 + levels - 1 - bit_level
        own_bit = position >> bit_level & 1
        kept_half = lax.dynamic_index_in_dim(merged, own_bit, axis_at, keepdims=False)
        sent_half = lax.dynamic_index_in_dim(merged, 1 - own_bit, axis_at, keepdims=False)
        partner_half = swapped(sent_half, "depth", bit_level)
        front_half = jnp.where(own_bit == 0, kept_half, partner_half)
        back_half = jnp.where(own_bit == 0, partner_half, kept_half)
        merged = blend_over(front_half, back_half)
    return jnp.concatenate([merged[:3], 1.0 - merged[3:]], 0)


def solution(mesh):
    in_specs = (P("depth", "rows", None), P("depth", "rows", None), P())
    out_specs = P(None, "rows", "depth")
    return jax.shard_map(shards, mesh=mesh, in_specs=in_specs, out_specs=out_specs, check_vma=False)
```

profile of v0, /device:TPU:0, one launch (start us, length us, event | category | flops | bytes accessed | tf_op | source)
XLA Modules:
  0.0 577.1 jit_solution(9992503607139209720)
XLA Ops:
  0.7 9.4 %copy.6 = f32[256,8,16,128]{3,2,1,0:T(8,128)S(1)} copy(f32[256,8,16,128]{3,1,2,0:T(8,128)} %bitcast.88) | data formatting | bytes 33554432
  10.1 2.1 bitcast_multiply_fusion.1
  12.5 5.0 collective-permute-start
  20.0 7.4 %broadcast_multiply_fusion = f32[16,128,2048]{2,1,0:T(8,128)S(1)} fusion(f32[16,128,2048]{2,1,0:T(8,128)} %param.5, f32[2048]{0:T(1024)S(1)} %broadcast_bitcast_fusion), kind=kLoop, calls=%fused_computation.40 | loop fusion | flops 4194304 | bytes 33562624 | tf_op jit(solution)/shard_map/mul | solution.py:87
  27.5 12.4 %collective-permute-done = f32[1,128,2048]{2,1,0:T(8,128)S(1)} collective-permute-done((f32[1,128,2048]{2,1,0:T(8,128)S(1)}, f32[1,128,2048]{2,1,0:T(8,128)S(1)}, u32[]{:S(2)}, u32[]{:S(2)}) %collective-permute-start) | collective-permute-done | bytes 1048608 | tf_op jit(solution)/shard_map/ppermute | solution.py:15
  39.9 5.5 collective-permute-done.1
  49.3 3.6 collective-permute-done.3
  52.8 25.4 %select_maximum_fusion = f32[18,130,2050]{2,1,0:T(8,128)} fusion(f32[18,1,2048]{2,1,0:T(1,128)} %collective-permute-done.3, f32[18,1,2048]{2,1,0:T(1,128)S(1)} %collective-permute-done.2, f32[1,128,2048]{2,1,0:T(8,128)} %copy-done.7, f32[16,128,2048]{2,1,0:T(8,128)} %copy-done, f32[1,128,2048]{2,1,0:T(8,128)} %copy-done.6), kind=kLoop, calls=%fused_computation.34 | loop fusion | flops 57564000 | bytes 38357280 | tf_op jit(solution)/shard_map/concatenate | solution.py:13
  78.3 377.9 %while.15 = (s32[]{:T(128)}, f32[3,128,2048]{2,1,0:T(8,128)S(1)}, f32[128,2048]{1,0:T(8,128)}, s32[16]{0:T(128)S(1)}, f32[18,130,2050]{2,1,0:T(8,128)}, /*index=...) while((s32[]{:T(128)}, f32[3,128,2048]{2,1,0:T(8,128)S(1)}, ...), condition=%wide.region_1.2_spmd.clone, body=%wide.region_0.1_spmd.clone.sunk | while | flops 20971528 | bytes 44040648 | solution.py:67
  81.4 13.3 %fusion.36 = (f32[128,2048]{1,0:T(8,128)}, f32[1,128,2048]{2,1,0:T(8,128)}, f32[1,128,2048]{2,1,0:T(8,128)}, f32[1,128,2048]{2,1,0:T(8,128)}) fusion(f32[18,130,2050]{2,1,0:T(8,128)} %get-tuple-element.239, s32[]{:T(128)S(6)} %add.294, s32[]{:T(128)S(6)} %add.295, s32[]{:T(128)S(6)} %add.296, s32[]{:T(128)S(6)} %select_n.109, s32[]{:T(128)S(6)} %add.297, ...), kind=kLoop, calls=%fused_computation.10.clone.1 | loop fusion | flops 12582912 | bytes 11534388 | tf_op jit(solution)/shard_map/while/body/eval_jaxpr/mul | solution.py:45
  94.7 5.0 fusion.37
  104.5 13.4 %fusion.36 = (f32[128,2048]{1,0:T(8,128)}, f32[1,128,2048]{2,1,0:T(8,128)}, f32[1,128,2048]{2,1,0:T(8,128)}, f32[1,128,2048]{2,1,0:T(8,128)}) fusion(f32[18,130,2050]{2,1,0:T(8,128)} %get-tuple-element.239, s32[]{:T(128)S(6)} %add.294, s32[]{:T(128)S(6)} %add.295, s32[]{:T(128)S(6)} %add.296, s32[]{:T(128)S(6)} %select_n.109, s32[]{:T(128)S(6)} %add.297, ...), kind=kLoop, calls=%fused_computation.10.clone.1 | loop fusion | flops 12582912 | bytes 11534388 | tf_op jit(solution)/shard_map/while/body/eval_jaxpr/mul | solution.py:45
  117.9 5.3 fusion.37
  128.0 13.6 %fusion.36 = (f32[128,2048]{1,0:T(8,128)}, f32[1,128,2048]{2,1,0:T(8,128)}, f32[1,128,2048]{2,1,0:T(8,128)}, f32[1,128,2048]{2,1,0:T(8,128)}) fusion(f32[18,130,2050]{2,1,0:T(8,128)} %get-tuple-element.239, s32[]{:T(128)S(6)} %add.294, s32[]{:T(128)S(6)} %add.295, s32[]{:T(128)S(6)} %add.296, s32[]{:T(128)S(6)} %select_n.109, s32[]{:T(128)S(6)} %add.297, ...), kind=kLoop, calls=%fused_computation.10.clone.1 | loop fusion | flops 12582912 | bytes 11534388 | tf_op jit(solution)/shard_map/while/body/eval_jaxpr/mul | solution.py:45
  141.6 5.3 fusion.37
  151.7 13.4 %fusion.36 = (f32[128,2048]{1,0:T(8,128)}, f32[1,128,2048]{2,1,0:T(8,128)}, f32[1,128,2048]{2,1,0:T(8,128)}, f32[1,128,2048]{2,1,0:T(8,128)}) fusion(f32[18,130,2050]{2,1,0:T(8,128)} %get-tuple-element.239, s32[]{:T(128)S(6)} %add.294, s32[]{:T(128)S(6)} %add.295, s32[]{:T(128)S(6)} %add.296, s32[]{:T(128)S(6)} %select_n.109, s32[]{:T(128)S(6)} %add.297, ...), kind=kLoop, calls=%fused_computation.10.clone.1 | loop fusion | flops 12582912 | bytes 11534388 | tf_op jit(solution)/shard_map/while/body/eval_jaxpr/mul | solution.py:45
  165.2 5.3 fusion.37
  175.3 13.5 %fusion.36 = (f32[128,2048]{1,0:T(8,128)}, f32[1,128,2048]{2,1,0:T(8,128)}, f32[1,128,2048]{2,1,0:T(8,128)}, f32[1,128,2048]{2,1,0:T(8,128)}) fusion(f32[18,130,2050]{2,1,0:T(8,128)} %get-tuple-element.239, s32[]{:T(128)S(6)} %add.294, s32[]{:T(128)S(6)} %add.295, s32[]{:T(128)S(6)} %add.296, s32[]{:T(128)S(6)} %select_n.109, s32[]{:T(128)S(6)} %add.297, ...), kind=kLoop, calls=%fused_computation.10.clone.1 | loop fusion | flops 12582912 | bytes 11534388 | tf_op jit(solution)/shard_map/while/body/eval_jaxpr/mul | solution.py:45
  188.8 5.3 fusion.37
  198.9 13.6 %fusion.36 = (f32[128,2048]{1,0:T(8,128)}, f32[1,128,2048]{2,1,0:T(8,128)}, f32[1,128,2048]{2,1,0:T(8,128)}, f32[1,128,2048]{2,1,0:T(8,128)}) fusion(f32[18,130,2050]{2,1,0:T(8,128)} %get-tuple-element.239, s32[]{:T(128)S(6)} %add.294, s32[]{:T(128)S(6)} %add.295, s32[]{:T(128)S(6)} %add.296, s32[]{:T(128)S(6)} %select_n.109, s32[]{:T(128)S(6)} %add.297, ...), kind=kLoop, calls=%fused_computation.10.clone.1 | loop fusion | flops 12582912 | bytes 11534388 | tf_op jit(solution)/shard_map/while/body/eval_jaxpr/mul | solution.py:45
  212.5 5.3 fusion.37
  222.6 13.8 %fusion.36 = (f32[128,2048]{1,0:T(8,128)}, f32[1,128,2048]{2,1,0:T(8,128)}, f32[1,128,2048]{2,1,0:T(8,128)}, f32[1,128,2048]{2,1,0:T(8,128)}) fusion(f32[18,130,2050]{2,1,0:T(8,128)} %get-tuple-element.239, s32[]{:T(128)S(6)} %add.294, s32[]{:T(128)S(6)} %add.295, s32[]{:T(128)S(6)} %add.296, s32[]{:T(128)S(6)} %select_n.109, s32[]{:T(128)S(6)} %add.297, ...), kind=kLoop, calls=%fused_computation.10.clone.1 | loop fusion | flops 12582912 | bytes 11534388 | tf_op jit(solution)/shard_map/while/body/eval_jaxpr/mul | solution.py:45
  236.4 5.3 fusion.37
  246.5 13.6 %fusion.36 = (f32[128,2048]{1,0:T(8,128)}, f32[1,128,2048]{2,1,0:T(8,128)}, f32[1,128,2048]{2,1,0:T(8,128)}, f32[1,128,2048]{2,1,0:T(8,128)}) fusion(f32[18,130,2050]{2,1,0:T(8,128)} %get-tuple-element.239, s32[]{:T(128)S(6)} %add.294, s32[]{:T(128)S(6)} %add.295, s32[]{:T(128)S(6)} %add.296, s32[]{:T(128)S(6)} %select_n.109, s32[]{:T(128)S(6)} %add.297, ...), kind=kLoop, calls=%fused_computation.10.clone.1 | loop fusion | flops 12582912 | bytes 11534388 | tf_op jit(solution)/shard_map/while/body/eval_jaxpr/mul | solution.py:45
  260.2 5.3 fusion.37
  270.3 13.4 %fusion.36 = (f32[128,2048]{1,0:T(8,128)}, f32[1,128,2048]{2,1,0:T(8,128)}, f32[1,128,2048]{2,1,0:T(8,128)}, f32[1,128,2048]{2,1,0:T(8,128)}) fusion(f32[18,130,2050]{2,1,0:T(8,128)} %get-tuple-element.239, s32[]{:T(128)S(6)} %add.294, s32[]{:T(128)S(6)} %add.295, s32[]{:T(128)S(6)} %add.296, s32[]{:T(128)S(6)} %select_n.109, s32[]{:T(128)S(6)} %add.297, ...), kind=kLoop, calls=%fused_computation.10.clone.1 | loop fusion | flops 12582912 | bytes 11534388 | tf_op jit(solution)/shard_map/while/body/eval_jaxpr/mul | solution.py:45
  283.7 5.3 fusion.37
  293.8 13.8 %fusion.36 = (f32[128,2048]{1,0:T(8,128)}, f32[1,128,2048]{2,1,0:T(8,128)}, f32[1,128,2048]{2,1,0:T(8,128)}, f32[1,128,2048]{2,1,0:T(8,128)}) fusion(f32[18,130,2050]{2,1,0:T(8,128)} %get-tuple-element.239, s32[]{:T(128)S(6)} %add.294, s32[]{:T(128)S(6)} %add.295, s32[]{:T(128)S(6)} %add.296, s32[]{:T(128)S(6)} %select_n.109, s32[]{:T(128)S(6)} %add.297, ...), kind=kLoop, calls=%fused_computation.10.clone.1 | loop fusion | flops 12582912 | bytes 11534388 | tf_op jit(solution)/shard_map/while/body/eval_jaxpr/mul | solution.py:45
  307.6 5.3 fusion.37
  317.7 13.7 %fusion.36 = (f32[128,2048]{1,0:T(8,128)}, f32[1,128,2048]{2,1,0:T(8,128)}, f32[1,128,2048]{2,1,0:T(8,128)}, f32[1,128,2048]{2,1,0:T(8,128)}) fusion(f32[18,130,2050]{2,1,0:T(8,128)} %get-tuple-element.239, s32[]{:T(128)S(6)} %add.294, s32[]{:T(128)S(6)} %add.295, s32[]{:T(128)S(6)} %add.296, s32[]{:T(128)S(6)} %select_n.109, s32[]{:T(128)S(6)} %add.297, ...), kind=kLoop, calls=%fused_computation.10.clone.1 | loop fusion | flops 12582912 | bytes 11534388 | tf_op jit(solution)/shard_map/while/body/eval_jaxpr/mul | solution.py:45
  331.4 5.3 fusion.37
  341.5 13.4 %fusion.36 = (f32[128,2048]{1,0:T(8,128)}, f32[1,128,2048]{2,1,0:T(8,128)}, f32[1,128,2048]{2,1,0:T(8,128)}, f32[1,128,2048]{2,1,0:T(8,128)}) fusion(f32[18,130,2050]{2,1,0:T(8,128)} %get-tuple-element.239, s32[]{:T(128)S(6)} %add.294, s32[]{:T(128)S(6)} %add.295, s32[]{:T(128)S(6)} %add.296, s32[]{:T(128)S(6)} %select_n.109, s32[]{:T(128)S(6)} %add.297, ...), kind=kLoop, calls=%fused_computation.10.clone.1 | loop fusion | flops 12582912 | bytes 11534388 | tf_op jit(solution)/shard_map/while/body/eval_jaxpr/mul | solution.py:45
  354.9 5.3 fusion.37
  365.0 13.4 %fusion.36 = (f32[128,2048]{1,0:T(8,128)}, f32[1,128,2048]{2,1,0:T(8,128)}, f32[1,128,2048]{2,1,0:T(8,128)}, f32[1,128,2048]{2,1,0:T(8,128)}) fusion(f32[18,130,2050]{2,1,0:T(8,128)} %get-tuple-element.239, s32[]{:T(128)S(6)} %add.294, s32[]{:T(128)S(6)} %add.295, s32[]{:T(128)S(6)} %add.296, s32[]{:T(128)S(6)} %select_n.109, s32[]{:T(128)S(6)} %add.297, ...), kind=kLoop, calls=%fused_computation.10.clone.1 | loop fusion | flops 12582912 | bytes 11534388 | tf_op jit(solution)/shard_map/while/body/eval_jaxpr/mul | solution.py:45
  378.4 5.3 fusion.37
  388.5 13.5 %fusion.36 = (f32[128,2048]{1,0:T(8,128)}, f32[1,128,2048]{2,1,0:T(8,128)}, f32[1,128,2048]{2,1,0:T(8,128)}, f32[1,128,2048]{2,1,0:T(8,128)}) fusion(f32[18,130,2050]{2,1,0:T(8,128)} %get-tuple-element.239, s32[]{:T(128)S(6)} %add.294, s32[]{:T(128)S(6)} %add.295, s32[]{:T(128)S(6)} %add.296, s32[]{:T(128)S(6)} %select_n.109, s32[]{:T(128)S(6)} %add.297, ...), kind=kLoop, calls=%fused_computation.10.clone.1 | loop fusion | flops 12582912 | bytes 11534388 | tf_op jit(solution)/shard_map/while/body/eval_jaxpr/mul | solution.py:45
  402.0 5.3 fusion.37
  412.1 13.5 %fusion.36 = (f32[128,2048]{1,0:T(8,128)}, f32[1,128,2048]{2,1,0:T(8,128)}, f32[1,128,2048]{2,1,0:T(8,128)}, f32[1,128,2048]{2,1,0:T(8,128)}) fusion(f32[18,130,2050]{2,1,0:T(8,128)} %get-tuple-element.239, s32[]{:T(128)S(6)} %add.294, s32[]{:T(128)S(6)} %add.295, s32[]{:T(128)S(6)} %add.296, s32[]{:T(128)S(6)} %select_n.109, s32[]{:T(128)S(6)} %add.297, ...), kind=kLoop, calls=%fused_computation.10.clone.1 | loop fusion | flops 12582912 | bytes 11534388 | tf_op jit(solution)/shard_map/while/body/eval_jaxpr/mul | solution.py:45
  425.6 5.3 fusion.37
  435.7 13.5 %fusion.36 = (f32[128,2048]{1,0:T(8,128)}, f32[1,128,2048]{2,1,0:T(8,128)}, f32[1,128,2048]{2,1,0:T(8,128)}, f32[1,128,2048]{2,1,0:T(8,128)}) fusion(f32[18,130,2050]{2,1,0:T(8,128)} %get-tuple-element.239, s32[]{:T(128)S(6)} %add.294, s32[]{:T(128)S(6)} %add.295, s32[]{:T(128)S(6)} %add.296, s32[]{:T(128)S(6)} %select_n.109, s32[]{:T(128)S(6)} %add.297, ...), kind=kLoop, calls=%fused_computation.10.clone.1 | loop fusion | flops 12582912 | bytes 11534388 | tf_op jit(solution)/shard_map/while/body/eval_jaxpr/mul | solution.py:45
  449.2 5.3 fusion.37
  456.2 3.8 concatenate.22
  459.9 4.9 constant_dynamic-update-slice_fusion.1
  467.0 7.8 %constant_dynamic-slice_fusion.1 = (f32[4,128,2,1,512]{4,3,2,1,0:T(1,128)S(1)}, f32[4,128,2,1,512]{4,3,2,1,0:T(1,128)S(1)}) fusion(f32[4,128,2,2,512]{4,3,2,1,0:T(2,128)} %constant_dynamic-update-slice_fusion, s32[]{:T(128)S(6)} %select_n.59, s32[]{:T(128)S(6)} %select_n.60), kind=kLoop, calls=%fused_computation.71 | loop fusion | bytes 8388616 | tf_op jit(solution)/shard_map/jit(dynamic_index_in_dim)/dynamic_slice | solution.py:102
  478.0 44.6 %collective-permute-done.4 = f32[4,128,2,512]{3,1,0,2:T(8,128)} collective-permute-done((f32[4,128,2,512]{3,1,0,2:T(8,128)}, f32[4,128,2,512]{3,1,0,2:T(8,128)}, u32[]{:S(2)}, u32[]{:S(2)}) %collective-permute-start.4) | collective-permute-done | bytes 2097184 | tf_op jit(solution)/shard_map/ppermute | solution.py:31
  522.6 2.5 bitcast_select_fusion.1
  525.8 2.6 collective-permute-start.5
  528.4 45.9 %collective-permute-done.5 = f32[4,128,512]{2,1,0:T(8,128)} collective-permute-done((f32[4,128,512]{2,1,0:T(8,128)S(1)}, f32[4,128,512]{2,1,0:T(8,128)}, u32[]{:S(2)}, u32[]{:S(2)}) %collective-permute-start.5) | collective-permute-done | bytes 1048608 | tf_op jit(solution)/shard_map/ppermute | solution.py:31
  (210 shorter events, 62.7 us)
Async XLA Ops:
  12.5 27.4 %collective-permute-start = (f32[1,128,2048]{2,1,0:T(8,128)S(1)}, f32[1,128,2048]{2,1,0:T(8,128)S(1)}, u32[]{:S(2)}, u32[]{:S(2)}) collective-permute-start(f32[1,128,2048]{2,1,0:T(8,128)S(1)} %slice.135), channel_id=1, source_target_pairs={{0,8},{8,16},{16,24},{1,9},{9,17},{17,25},{2,10},{10,18},{18,26},{... | collective-permute-start | bytes 3145736 | tf_op jit(solution)/shard_map/ppermute | solution.py:15
  18.7 26.7 %collective-permute-start.1 = (f32[1,128,2048]{2,1,0:T(8,128)}, f32[1,128,2048]{2,1,0:T(8,128)S(1)}, u32[]{:S(2)}, u32[]{:S(2)}) collective-permute-start(f32[1,128,2048]{2,1,0:T(8,128)} %slice.137), channel_id=1, source_target_pairs={{8,0},{16,8},{24,16},{9,1},{17,9},{25,17},{10,2},{18,10},{26,18},{... | collective-permute-start | bytes 3145736 | tf_op jit(solution)/shard_map/ppermute | solution.py:17
  27.4 19.0 %copy-start = (f32[16,128,2048]{2,1,0:T(8,128)}, f32[16,128,2048]{2,1,0:T(8,128)S(1)}, u32[]{:S(2)}) copy-start(f32[16,128,2048]{2,1,0:T(8,128)S(1)} %broadcast_multiply_fusion) | copy-start | bytes 50331652
  39.9 6.5 %copy-start.6 = (f32[1,128,2048]{2,1,0:T(8,128)}, f32[1,128,2048]{2,1,0:T(8,128)S(1)}, u32[]{:S(2)}) copy-start(f32[1,128,2048]{2,1,0:T(8,128)S(1)} %collective-permute-done) | copy-start | bytes 3145732
  46.4 2.8 collective-permute-start.2
  47.7 5.1 collective-permute-start.3
  49.2 29.1 %copy-start.8 = (f32[2,4]{1,0:T(2,128)S(1)}, f32[2,4]{1,0:T(2,128)}, u32[]{:S(2)}) copy-start(f32[2,4]{1,0:T(2,128)} %param.7) | copy-start | bytes 100
  117.9 5.3 copy-start.1
  117.9 5.3 copy-start.2
  117.9 5.3 copy-start.3
  141.6 5.3 copy-start.1
  141.6 5.3 copy-start.2
  141.6 5.3 copy-start.3
  165.1 5.3 copy-start.1
  165.1 5.3 copy-start.2
  165.1 5.3 copy-start.3
  188.7 5.3 copy-start.1
  188.7 5.3 copy-start.2
  188.7 5.3 copy-start.3
  212.5 5.3 copy-start.1
  212.5 5.3 copy-start.2
  212.5 5.3 copy-start.3
  236.4 5.3 copy-start.1
  236.4 5.3 copy-start.2
  236.4 5.3 copy-start.3
  260.1 5.3 copy-start.1
  260.1 5.3 copy-start.2
  260.1 5.3 copy-start.3
  283.6 5.3 copy-start.1
  283.6 5.3 copy-start.2
  307.5 5.3 copy-start.1
  307.6 5.3 copy-start.2
  307.6 5.3 copy-start.3
  331.3 5.3 copy-start.1
  331.4 5.3 copy-start.2
  331.4 5.3 copy-start.3
  354.8 5.3 copy-start.1
  354.8 5.3 copy-start.2
  378.3 5.3 copy-start.1
  378.3 5.3 copy-start.2
  402.0 5.3 copy-start.1
  402.0 5.3 copy-start.2
  425.6 5.3 copy-start.1
  425.6 5.3 copy-start.2
  449.2 5.3 copy-start.1
  449.2 5.3 copy-start.2
  476.5 46.1 %collective-permute-start.4 = (f32[4,128,2,512]{3,1,0,2:T(8,128)}, f32[4,128,2,512]{3,1,0,2:T(8,128)}, u32[]{:S(2)}, u32[]{:S(2)}) collective-permute-start(f32[4,128,2,512]{3,1,0,2:T(8,128)} %bitcast.64), channel_id=1, source_target_pairs={{0,8},{8,0},{16,24},{24,16},{1,9},{9,1},{17,25},{25,17},{2,10},{10... | collective-permute-start | bytes 6291464 | tf_op jit(solution)/shard_map/ppermute | solution.py:31
  525.8 48.5 %collective-permute-start.5 = (f32[4,128,512]{2,1,0:T(8,128)S(1)}, f32[4,128,512]{2,1,0:T(8,128)}, u32[]{:S(2)}, u32[]{:S(2)}) collective-permute-start(f32[4,128,512]{2,1,0:T(8,128)S(1)} %fusion.24), channel_id=1, source_target_pairs={{0,16},{16,0},{8,24},{24,8},{1,17},{17,1},{9,25},{25,9},{2,18},{18... | collective-permute-start | bytes 3145736 | tf_op jit(solution)/shard_map/ppermute | solution.py:31
  (27 other events, 137.4 us)
where the time goes:
time: 583 us; the launch traced here: 577 us
  other arithmetic  369 us (63%)
  waiting for transfers between devices  112 us (19%)
  local copies, waits for them, and re-layouts  52.1 us (9%)
  loops' own time  30.7 us (5%)
  starting transfers between devices  13.2 us (2%)
    mul x16, other arithmetic, shade(): return (opacity * lighting * colors, opacity)  216 us
    ppermute x2, waiting for transfers between devices, swapped(): return lax.ppermute(block, axis, route)  90.5 us
    mul x16, other arithmetic, advance(): return ((color_sum + transmit * shaded, transmit * (1.0 - opacity)), None)  84.3 us
    another operation x1, loops' own time, march(): lax.scan(advance, start_state, jnp.arange(depth_count, dtype=jnp.int32))  30.7 us
    add x16, other arithmetic, advance(): return ((color_sum + transmit * shaded, transmit * (1.0 - opacity)), None)  25.9 us
    concatenate x1, other arithmetic, extended_2(): jnp.concatenate([lax.ppermute(tail, axis, [(i, (i + 1) % count) for i in...  25.4 us
    unnamed x12, local copies, waits for them, and re-layouts  14.3 us
    ppermute x2, waiting for transfers between devices, extended_2(): lax.ppermute(tail, axis, [(i, (i + 1) % count) for i in range(ends)])  12.4 us
  transfers between devices with their start and end apart: 6, of which 5 were waited for; matrix products, arithmetic and copies ran while one was open for 1% of the time, Pallas kernels for 0%

commit v1 on v0

v1 whole, which is shorter than its diff:
```python
import functools
import jax
import jax.numpy as jnp
from jax import lax
from jax.experimental import pallas as pl
from jax.experimental.pallas import tpu as pltpu
from jax.sharding import PartitionSpec as P

OCCUPIED_MOST = 12
PAD = 8
ROWS_AT_ONCE = 16
LOG2_E = 1.4426950408889634
SMEM = pl.BlockSpec(memory_space=pltpu.SMEM)
VMEM = pl.BlockSpec(memory_space=pltpu.VMEM)
ANY = pl.BlockSpec(memory_space=pl.ANY)


def pack_kernel(width, flags, density, head, tail, first_row, last_row, top, bottom, plane_sem, row_sem):
    depth_cells, row_cells, _ = density.shape
    block_count = flags.shape[0]
    slots = head.shape[0] // row_cells
    top_copy = pltpu.make_async_copy(density.at[:, 0:8, :], top, row_sem.at[0])
    bottom_copy = pltpu.make_async_copy(density.at[:, row_cells - 8 : row_cells, :], bottom, row_sem.at[1])
    top_copy.start()
    bottom_copy.start()

    def copies(block, slot):
        columns = pl.ds(pl.multiple_of(block * width, width), width)
        rows = pl.ds(pl.multiple_of(slot * row_cells, row_cells), row_cells)
        return (
            pltpu.make_async_copy(density.at[0, :, columns], head.at[rows, :], plane_sem.at[0, slot]),
            pltpu.make_async_copy(density.at[depth_cells - 1, :, columns], tail.at[rows, :], plane_sem.at[1, slot]),
        )

    def begin(block, slot):
        wanted = jnp.logical_and(flags[block] > 0, slot < slots)

        @pl.when(wanted)
        def _():
            for copy in copies(block, slot):
                copy.start()

        return slot + wanted.astype(jnp.int32)

    used = lax.fori_loop(0, block_count, begin, jnp.int32(0))
    top_copy.wait()
    bottom_copy.wait()

    def edge(block, carry):
        columns = pl.ds(pl.multiple_of(block * width, width), width)
        flag = flags[block].astype(jnp.float32)
        for z in range(depth_cells):
            first_row[pl.ds(z, 1), columns] = top[z, 0:1, columns] * flag
            last_row[pl.ds(z, 1), columns] = bottom[z, 7:8, columns] * flag
        return carry

    lax.fori_loop(0, block_count, edge, 0)

    def end(slot, carry):
        for copy in copies(0, slot):
            copy.wait()
        return carry

    lax.fori_loop(0, used, end, 0)


def pack(density, flags, width):
    depth_cells, row_cells, col_cells = density.shape
    slots = min(OCCUPIED_MOST, flags.shape[0])
    plane = jax.ShapeDtypeStruct((slots * row_cells, width), jnp.float32)
    row = jax.ShapeDtypeStruct((depth_cells, col_cells), jnp.float32)
    return pl.pallas_call(
        functools.partial(pack_kernel, width),
        out_shape=(plane, plane, row, row),
        in_specs=[SMEM, ANY],
        out_specs=[VMEM] * 4,
        scratch_shapes=[
            pltpu.VMEM((depth_cells, 8, col_cells), jnp.float32),
            pltpu.VMEM((depth_cells, 8, col_cells), jnp.float32),
            pltpu.SemaphoreType.DMA((2, slots)),
            pltpu.SemaphoreType.DMA((2,)),
        ],
        name="pack",
    )(flags, density)


def shade_kernel(
    first_at,
    piece_total,
    width,
    ray_step,
    flags,
    low_flags,
    high_flags,
    turned,
    transfer,
    density,
    low_plane,
    high_plane,
    above,
    below,
    out,
    vol,
    block_sem,
    plane_sem,
):
    depth_cells, row_cells, _ = density.shape
    block_count = flags.shape[0]
    piece_blocks = block_count // piece_total
    piece_count = out.shape[0]
    own = piece_count * piece_blocks
    zero_slot = own + 2
    backward = turned[0] > 0
    first_piece = jnp.where(backward, first_at, piece_total - first_at - piece_count)
    first_block = first_piece * piece_blocks
    body = pl.ds(PAD, row_cells)

    def block_of(slot):
        return first_block + slot - 1

    def occupied(block):
        inside = jnp.logical_and(block >= 0, block < block_count)
        return jnp.logical_and(inside, flags[jnp.clip(block, 0, block_count - 1)] > 0)

    def block_copy(slot):
        block = jnp.clip(block_of(slot), 0, block_count - 1)
        columns = pl.ds(pl.multiple_of(block * width, width), width)
        return pltpu.make_async_copy(
            density.at[:, :, columns], vol.at[slot, pl.ds(1, depth_cells), body, :], block_sem.at[slot]
        )

    def low_copy(slot, rank):
        rows = pl.ds(pl.multiple_of(rank * row_cells, row_cells), row_cells)
        return pltpu.make_async_copy(low_plane.at[rows, :], vol.at[slot, 0, body, :], plane_sem.at[0, slot])

    def high_copy(slot, rank):
        rows = pl.ds(pl.multiple_of(rank * row_cells, row_cells), row_cells)
        return pltpu.make_async_copy(
            high_plane.at[rows, :], vol.at[slot, depth_cells + 1, body, :], plane_sem.at[1, slot]
        )

    def begin_block(slot, carry):
        @pl.when(occupied(block_of(slot)))
        def _():
            block_copy(slot).start()

        return carry

    lax.fori_loop(0, own + 2, begin_block, 0)

    def begin_plane(block, ranks):
        low_rank, high_rank = ranks
        slot = block - first_block + 1
        mine = jnp.logical_and(jnp.logical_and(slot >= 1, slot <= own), flags[block] > 0)
        low = low_flags[block] > 0
        high = high_flags[block] > 0

        @pl.when(jnp.logical_and(mine, low))
        def _():
            low_copy(slot, low_rank).start()

        @pl.when(jnp.logical_and(mine, high))
        def _():
            high_copy(slot, high_rank).start()

        return (low_rank + low.astype(jnp.int32), high_rank + high.astype(jnp.int32))

    lax.fori_loop(0, block_count, begin_plane, (jnp.int32(0), jnp.int32(0)))

    def clear(z, carry):
        vol[zero_slot, z, body, :] = jnp.zeros((row_cells, width), jnp.float32)
        return carry

    lax.fori_loop(1, depth_cells + 1, clear, 0)

    def arrive(slot):
        @pl.when(occupied(block_of(slot)))
        def _():
            block_copy(slot).wait()

    arrive(0)
    arrive(1)

    def visit(slot, carry):
        block = block_of(slot)
        piece = block // piece_blocks - first_piece
        place = jnp.where(backward, piece, piece_count - 1 - piece)
        columns = pl.ds(pl.multiple_of(lax.rem(block, piece_blocks) * width, width), width)
        arrive(slot + 1)

        @pl.when(jnp.logical_not(occupied(block)))
        def _():
            for channel in range(4):
                out[place, channel, :, columns] = jnp.full((row_cells, width), 1.0 if channel == 3 else 0.0, jnp.float32)

        @pl.when(occupied(block))
        def _():
            left = jnp.where(occupied(block - 1), slot - 1, zero_slot)
            right = jnp.where(occupied(block + 1), slot + 1, zero_slot)
            source = pl.ds(pl.multiple_of(block * width, width), width)
            for z in range(depth_cells):
                vol[slot, z + 1, pl.ds(PAD - 1, 1), :] = above[pl.ds(z, 1), source]
                vol[slot, z + 1, pl.ds(PAD + row_cells, 1), :] = below[pl.ds(z, 1), source]
            for side, side_flags, plane_copy in ((0, low_flags, low_copy), (1, high_flags, high_copy)):
                near = side_flags[block] > 0

                @pl.when(near)
                def _():
                    plane_copy(slot, 0).wait()

                @pl.when(jnp.logical_not(near))
                def _():
                    vol[slot, side * (depth_cells + 1), body, :] = jnp.zeros((row_cells, width), jnp.float32)

            march(slot, left, right, place, columns)

        return carry

    def march(slot, left, right, place, columns):
        rows_at_once = ROWS_AT_ONCE
        shape = (rows_at_once, width)
        lane = lax.broadcasted_iota(jnp.int32, shape, 1)
        at_first = lane == 0
        at_last = lane == width - 1
        slopes = [transfer[0, channel] * 0.5 for channel in range(3)]
        offsets = [transfer[1, channel] * 0.5 for channel in range(3)]
        decay_slope = transfer[0, 3] * LOG2_E
        decay_offset = transfer[1, 3] * LOG2_E

        def chunk(at, carry):
            start = pl.multiple_of(PAD + at * rows_at_once, 8)
            rows = pl.ds(start, rows_at_once)
            previous = vol[slot, 0, rows, :]
            center = vol[slot, 1, rows, :]
            transmit = jnp.ones(shape, jnp.float32)
            plain = jnp.zeros(shape, jnp.float32)
            tinted = [jnp.zeros(shape, jnp.float32) for _ in range(3)]
            for z in range(1, depth_cells + 1):
                following = vol[slot, z + 1, rows, :]
                diff_z = following - previous
                diff_y = vol[slot, z, pl.ds(start + 1, rows_at_once), :] - vol[slot, z, pl.ds(start - 1, rows_at_once), :]
                right_side = pltpu.roll(jnp.where(at_first, vol[right, z, rows, :], center), width - 1, 1)
                left_side = pltpu.roll(jnp.where(at_last, vol[left, z, rows, :], center), 1, 1)
                diff_x = right_side - left_side
                facing = jnp.abs(diff_x + 0.9375 * diff_y + 0.75 * diff_z)
                norm = lax.rsqrt(diff_x * diff_x + diff_y * diff_y + (diff_z * diff_z + 4.0))
                lighting = facing * norm + (0.3 / 0.448)
                soft = jnp.log(1.0 + jnp.exp2(decay_slope * center + decay_offset))
                passed = transmit * jnp.exp2((center * (-ray_step * LOG2_E)) * soft)
                weight = (transmit - passed) * lighting
                transmit = passed
                plain = plain + weight
                for channel in range(3):
                    tinted[channel] = tinted[channel] + weight * jnp.tanh(slopes[channel] * center + offsets[channel])
                previous, center = center, following
            target = pl.ds(pl.multiple_of(at * rows_at_once, 8), rows_at_once)
            for channel in range(3):
                out[place, channel, target, columns] = 0.224 * (plain + tinted[channel])
            out[place, 3, target, columns] = transmit
            return carry

        lax.fori_loop(0, row_cells // rows_at_once, chunk, 0)

    lax.fori_loop(1, own + 1, visit, 0)


def shade(first_at, piece_count, piece_total, ray_step, flags, low_flags, high_flags, turned, transfer, density, low_plane, high_plane, above, below):
    depth_cells, row_cells, col_cells = density.shape
    block_count = flags.shape[0]
    width = col_cells // block_count
    own = piece_count * (block_count // piece_total)
    cells = own * depth_cells * row_cells * width
    return pl.pallas_call(
        functools.partial(shade_kernel, first_at, piece_total, width, ray_step),
        out_shape=jax.ShapeDtypeStruct((piece_count, 4, row_cells, col_cells // piece_total), jnp.float32),
        in_specs=[SMEM] * 5 + [ANY] * 3 + [VMEM] * 2,
        out_specs=VMEM,
        scratch_shapes=[
            pltpu.VMEM((own + 3, depth_cells + 2, row_cells + 2 * PAD, width), jnp.float32),
            pltpu.SemaphoreType.DMA((own + 2,)),
            pltpu.SemaphoreType.DMA((2, own + 2)),
        ],
        compiler_params=pltpu.CompilerParams(vmem_limit_bytes=48 << 20),
        cost_estimate=pl.CostEstimate(flops=60 * cells, bytes_accessed=4 * cells, transcendentals=7 * cells),
        name=f"shade_{first_at}",
    )(flags, low_flags, high_flags, turned, transfer, density, low_plane, high_plane, above, below)


def blend_over(front_part, back_part):
    color_sum = front_part[:3] + front_part[3:] * back_part[:3]
    transmit = front_part[3:] * back_part[3:]
    return jnp.concatenate([color_sum, transmit], 0)


def clear_unless(part, present):
    return jnp.concatenate([part[:3], jnp.where(present, part[3:], 1.0)], 0)


def shards(density, occupancy, transfer):
    depth_cells, row_cells, col_cells = density.shape
    flags = occupancy.reshape(-1)
    block_count = flags.shape[0]
    width = col_cells // block_count
    count = lax.axis_size("depth")
    slabs = lax.axis_size("rows")
    position = lax.axis_index("depth")
    ray_step = 2.0 / (depth_cells * count)
    later = [(i, i + 1) for i in range(count - 1)]
    sooner = [(i + 1, i) for i in range(count - 1)]

    head, tail, first_row, last_row = pack(density, flags, width)
    low_plane = lax.ppermute(tail, "depth", later)
    high_plane = lax.ppermute(head, "depth", sooner)
    low_flags = lax.ppermute(flags, "depth", later)
    high_flags = lax.ppermute(flags, "depth", sooner)
    above = lax.ppermute(last_row, "rows", [(i, i + 1) for i in range(slabs - 1)])
    below = lax.ppermute(first_row, "rows", [(i + 1, i) for i in range(slabs - 1)])
    backward = position >= count // 2
    turned = backward.astype(jnp.int32).reshape(1)
    args = (flags, low_flags, high_flags, turned, transfer, density, low_plane, high_plane, above, below)
    first = shade(0, 1, count, ray_step, *args)[0]
    rest = shade(1, count - 1, count, ray_step, *args)

    def own_piece(piece):
        at = jnp.where(backward, piece, count - 1 - piece)
        at = jnp.clip(at, 0, count - 1)
        other = lax.dynamic_index_in_dim(rest, jnp.maximum(at - 1, 0), 0, keepdims=False)
        return jnp.where(at == 0, first, other)

    front = back = None
    for step in range(count - 1):
        up_piece = own_piece(count - 1 - step + position) if step else first
        down_piece = own_piece(step + position - (count - 1)) if step else first
        if step:
            up_piece = blend_over(clear_unless(front, position > 0), up_piece)
            down_piece = blend_over(down_piece, clear_unless(back, position < count - 1))
        ups = [(i, i + 1) for i in range(step + 1)]
        downs = [(count - 1 - i, count - 2 - i) for i in range(step + 1)]
        front = lax.ppermute(up_piece, "depth", ups)
        back = lax.ppermute(down_piece, "depth", downs)
    merged = blend_over(own_piece(position), clear_unless(back, position < count - 1))
    merged = blend_over(clear_unless(front, position > 0), merged)
    return jnp.concatenate([merged[:3], 1.0 - merged[3:]], 0)


def solution(mesh):
    in_specs = (P("depth", "rows", None), P("depth", "rows", None), P())
    out_specs = P(None, "rows", "depth")
    return jax.shard_map(shards, mesh=mesh, in_specs=in_specs, out_specs=out_specs, check_vma=False)
```

time: 583 us -> 122 us (0.21)
  the two profiles are of different devices: /device:TPU:0 before, /device:TPU:10 now
where the time goes in v1:
time: 122 us; the launch traced here: 119 us
  waiting for transfers between devices  66.5 us (55%)
  starting transfers between devices  29.9 us (25%)
  Pallas kernels  16.8 us (14%)
  other arithmetic  5.78 us (5%)
    ppermute x3, waiting for transfers between devices, shards(): back = lax.ppermute(down_piece, 'depth', downs)  28.9 us
    ppermute x3, waiting for transfers between devices, shards(): front = lax.ppermute(up_piece, 'depth', ups)  27.7 us
    pallas_call x2, Pallas kernels, shade(): pl.pallas_call(functools.partial(shade_kernel, first_at, piece_total, wid...  12.8 us
    ppermute x3, starting transfers between devices, shards(): front = lax.ppermute(up_piece, 'depth', ups)  8.11 us
    ppermute x1, waiting for transfers between devices, shards(): low_flags = lax.ppermute(flags, 'depth', later)  6.4 us
    ppermute x3, starting transfers between devices, shards(): back = lax.ppermute(down_piece, 'depth', downs)  4.87 us
    pallas_call x1, Pallas kernels, pack(): pl.pallas_call(functools.partial(pack_kernel, width), out_shape=(plane, p...  4.05 us
    ppermute x1, starting transfers between devices, shards(): lax.ppermute(first_row, 'rows', [(i + 1, i) for i in range(slabs - 1)])  3.64 us
  transfers between devices with their start and end apart: 12, of which 7 were waited for; matrix products, arithmetic and copies ran while one was open for 4% of the time, Pallas kernels for 7%

profile of v1, /device:TPU:10, one launch (start us, length us, event | category | flops | bytes accessed | tf_op | source)
XLA Modules:
  0.0 119.3 jit_solution(2001435600168013091)
XLA Ops:
  0.0 0.0 copy-start
  0.0 0.0 copy-start.1
  0.0 4.0 %pack.1 = (f32[1536,128]{1,0:T(8,128)}, f32[1536,128]{1,0:T(8,128)}, f32[16,2048]{1,0:T(8,128)}, f32[16,2048]{1,0:T(8,128)}) custom-call(s32[16]{0:T(128)} %bitcast.32, f32[16,128,2048]{2,1,0:T(8,128)} %density.5), custom_call_target="tpu_custom_call" | custom-call | tf_op jit(solution)/shard_map/pack/pallas_call | solution.py:72
  4.1 3.6 %collective-permute-start.2 = (f32[1536,128]{1,0:T(8,128)}, f32[1536,128]{1,0:T(8,128)S(1)}, u32[]{:S(2)}, u32[]{:S(2)}) collective-permute-start(f32[1536,128]{1,0:T(8,128)} %get-tuple-element.9), channel_id=1, source_target_pairs={{0,8},{8,16},{16,24},{1,9},{9,17},{17,25},{2,10},{10,18},{18,26},{... | collective-permute-start | bytes 2359304 | tf_op jit(solution)/shard_map/ppermute | solution.py:312
  7.7 2.3 %collective-permute-start.3 = (f32[1536,128]{1,0:T(8,128)}, f32[1536,128]{1,0:T(8,128)S(1)}, u32[]{:S(2)}, u32[]{:S(2)}) collective-permute-start(f32[1536,128]{1,0:T(8,128)} %get-tuple-element.10), channel_id=1, source_target_pairs={{8,0},{16,8},{24,16},{9,1},{17,9},{25,17},{10,2},{18,10},{26,18},{... | collective-permute-start | bytes 2359304 | tf_op jit(solution)/shard_map/ppermute | solution.py:313
  10.0 1.9 %collective-permute-start.4 = (f32[16,2048]{1,0:T(8,128)}, f32[16,2048]{1,0:T(8,128)S(1)}, u32[]{:S(2)}, u32[]{:S(2)}) collective-permute-start(f32[16,2048]{1,0:T(8,128)} %get-tuple-element.11), channel_id=1, source_target_pairs={{0,1},{1,2},{2,3},{3,4},{4,5},{5,6},{6,7},{8,9},{9,10},{10,11},{11... | collective-permute-start | bytes 393224 | tf_op jit(solution)/shard_map/ppermute | solution.py:316
  11.9 3.6 %collective-permute-start.5 = (f32[16,2048]{1,0:T(8,128)}, f32[16,2048]{1,0:T(8,128)S(1)}, u32[]{:S(2)}, u32[]{:S(2)}) collective-permute-start(f32[16,2048]{1,0:T(8,128)} %get-tuple-element.12), channel_id=1, source_target_pairs={{1,0},{2,1},{3,2},{4,3},{5,4},{6,5},{7,6},{9,8},{10,9},{11,10},{12... | collective-permute-start | bytes 393224 | tf_op jit(solution)/shard_map/ppermute | solution.py:317
  15.5 0.0 copy-done
  15.6 3.6 %collective-permute-start = (s32[16]{0:T(128)S(1)}, s32[16]{0:T(128)S(1)}, u32[]{:S(2)}, u32[]{:S(2)}) collective-permute-start(s32[16]{0:T(128)S(1)} %bitcast.33), channel_id=1, source_target_pairs={{0,8},{8,16},{16,24},{1,9},{9,17},{17,25},{2,10},{10,18},{18,26},{... | collective-permute-start | bytes 200 | tf_op jit(solution)/shard_map/ppermute | solution.py:314
  19.2 6.4 %collective-permute-done.low_flags = s32[16]{0:T(128)S(1)} collective-permute-done((s32[16]{0:T(128)S(1)}, s32[16]{0:T(128)S(1)}, u32[]{:S(2)}, u32[]{:S(2)}) %collective-permute-start) | collective-permute-done | bytes 96 | tf_op jit(solution)/shard_map/ppermute | solution.py:314
  25.5 1.9 %collective-permute-start.1 = (s32[16]{0:T(128)S(1)}, s32[16]{0:T(128)S(1)}, u32[]{:S(2)}, u32[]{:S(2)}) collective-permute-start(s32[16]{0:T(128)S(1)} %bitcast.34), channel_id=1, source_target_pairs={{8,0},{16,8},{24,16},{9,1},{17,9},{25,17},{10,2},{18,10},{26,18},{... | collective-permute-start | bytes 200 | tf_op jit(solution)/shard_map/ppermute | solution.py:315
  27.5 3.5 %collective-permute-done.1.high_flags = s32[16]{0:T(128)S(1)} collective-permute-done((s32[16]{0:T(128)S(1)}, s32[16]{0:T(128)S(1)}, u32[]{:S(2)}, u32[]{:S(2)}) %collective-permute-start.1) | collective-permute-done | bytes 96 | tf_op jit(solution)/shard_map/ppermute | solution.py:315
  31.0 0.0 collective-permute-done.4.above
  31.0 0.0 collective-permute-done.5.below
  31.0 0.0 collective-permute-done.2.low_plane
  31.0 0.0 collective-permute-done.3.high_plane
  31.0 0.0 copy-done.1
  31.0 4.3 %shade_0.1 = f32[1,4,128,512]{3,2,1,0:T(8,128)S(1)} custom-call(s32[16]{0:T(128)S(1)} %bitcast.35, s32[16]{0:T(128)S(1)} %collective-permute-done.low_flags, s32[16]{0:T(128)S(1)} %collective-permute-done.1.high_flags, s32[1]{0:T(128)} %bitcast.1.turned, f32[2,4]{1,0:T(2,128)S(1)} %copy-done.1, f32[16,128,2048]{2,1,0:T(8,128)} %density.5, ...), custom_call_target="tpu_custom_call" | custom-call | flops 62914560 | bytes 4194304 | tf_op jit(solution)/shard_map/shade_0/pallas_call | solution.py:273
  35.4 1.7 %collective-permute-start.9 = (f32[4,128,512]{2,1,0:T(8,128)S(1)}, f32[4,128,512]{2,1,0:T(8,128)}, u32[]{:S(2)}, u32[]{:S(2)}) collective-permute-start(f32[4,128,512]{2,1,0:T(8,128)S(1)} %bitcast.30), channel_id=1, source_target_pairs={{24,16},{25,17},{26,18},{27,19},{28,20},{29,21},{30,22},{31,23}} | collective-permute-start | bytes 3145736 | tf_op jit(solution)/shard_map/ppermute | solution.py:340
  37.0 1.3 %collective-permute-start.6 = (f32[4,128,512]{2,1,0:T(8,128)S(1)}, f32[4,128,512]{2,1,0:T(8,128)S(1)}, u32[]{:S(2)}, u32[]{:S(2)}) collective-permute-start(f32[4,128,512]{2,1,0:T(8,128)S(1)} %bitcast.31), channel_id=1, source_target_pairs={{0,8},{1,9},{2,10},{3,11},{4,12},{5,13},{6,14},{7,15}} | collective-permute-start | bytes 3145736 | tf_op jit(solution)/shard_map/ppermute | solution.py:339
  38.3 8.5 %shade_1.1 = f32[3,4,128,512]{3,2,1,0:T(8,128)S(1)} custom-call(s32[16]{0:T(128)S(1)} %bitcast.36, s32[16]{0:T(128)S(1)} %collective-permute-done.low_flags, s32[16]{0:T(128)S(1)} %collective-permute-done.1.high_flags, s32[1]{0:T(128)} %bitcast.1.turned, f32[2,4]{1,0:T(2,128)S(1)} %copy-done.1, f32[16,128,2048]{2,1,0:T(8,128)} %density.5, ...), custom_call_target="tpu_custom_call" | custom-call | flops 188743680 | bytes 12582912 | tf_op jit(solution)/shard_map/shade_1/pallas_call | solution.py:273
  46.8 1.0 bitcast_select_fusion.4
  47.8 0.0 collective-permute-done.9
  47.8 1.0 slice_bitcast_fusion
  48.8 1.3 %fusion.4 = f32[3,128,512]{2,1,0:T(8,128)S(1)} fusion(f32[4,128,512]{2,1,0:T(8,128)} %collective-permute-done.9, f32[4,128,512]{2,1,0:T(8,128)S(1)} %get-tuple-element.14, f32[128,512]{1,0:T(8,128)S(1)} %get-tuple-element.27), kind=kLoop, calls=%fused_computation.17 | loop fusion | flops 393216 | bytes 2621440 | tf_op jit(solution)/shard_map/add | solution.py:290
  50.1 0.1 pad_maximum_fusion.2
  50.2 1.3 %collective-permute-start.10 = (f32[4,128,512]{2,1,0:T(8,128)S(1)}, f32[4,128,512]{2,1,0:T(8,128)S(1)}, u32[]{:S(2)}, u32[]{:S(2)}) collective-permute-start(f32[4,128,512]{2,1,0:T(8,128)S(1)} %pad_maximum_fusion.2), channel_id=1, source_target_pairs={{24,16},{16,8},{25,17},{17,9},{26,18},{18,10},{27,19},{19,11},{28,... | collective-permute-start | bytes 3145736 | tf_op jit(solution)/shard_map/ppermute | solution.py:340
  51.5 14.1 %collective-permute-done.6 = f32[4,128,512]{2,1,0:T(8,128)S(1)} collective-permute-done((f32[4,128,512]{2,1,0:T(8,128)S(1)}, f32[4,128,512]{2,1,0:T(8,128)S(1)}, u32[]{:S(2)}, u32[]{:S(2)}) %collective-permute-start.6) | collective-permute-done | bytes 1048608 | tf_op jit(solution)/shard_map/ppermute | solution.py:339
  65.6 0.2 fusion.6
  65.8 0.1 pad_maximum_fusion
  65.9 4.6 %collective-permute-start.7 = (f32[4,128,512]{2,1,0:T(8,128)S(1)}, f32[4,128,512]{2,1,0:T(8,128)S(1)}, u32[]{:S(2)}, u32[]{:S(2)}) collective-permute-start(f32[4,128,512]{2,1,0:T(8,128)S(1)} %pad_maximum_fusion), channel_id=1, source_target_pairs={{0,8},{8,16},{1,9},{9,17},{2,10},{10,18},{3,11},{11,19},{4,12},{12... | collective-permute-start | bytes 3145736 | tf_op jit(solution)/shard_map/ppermute | solution.py:339
  70.5 16.8 %collective-permute-done.10 = f32[4,128,512]{2,1,0:T(8,128)S(1)} collective-permute-done((f32[4,128,512]{2,1,0:T(8,128)S(1)}, f32[4,128,512]{2,1,0:T(8,128)S(1)}, u32[]{:S(2)}, u32[]{:S(2)}) %collective-permute-start.10) | collective-permute-done | bytes 1048608 | tf_op jit(solution)/shard_map/ppermute | solution.py:340
  87.4 0.2 fusion.3
  87.6 0.1 pad_maximum_fusion.3
  87.7 1.9 %collective-permute-start.11 = (f32[4,128,512]{2,1,0:T(8,128)S(1)}, f32[4,128,512]{2,1,0:T(8,128)S(1)}, u32[]{:S(2)}, u32[]{:S(2)}) collective-permute-start(f32[4,128,512]{2,1,0:T(8,128)S(1)} %pad_maximum_fusion.3), channel_id=1, source_target_pairs={{24,16},{16,8},{8,0},{25,17},{17,9},{9,1},{26,18},{18,10},{10,2},{... | collective-permute-start | bytes 3145736 | tf_op jit(solution)/shard_map/ppermute | solution.py:340
  89.6 2.5 %collective-permute-done.7 = f32[4,128,512]{2,1,0:T(8,128)S(1)} collective-permute-done((f32[4,128,512]{2,1,0:T(8,128)S(1)}, f32[4,128,512]{2,1,0:T(8,128)S(1)}, u32[]{:S(2)}, u32[]{:S(2)}) %collective-permute-start.7) | collective-permute-done | bytes 1048608 | tf_op jit(solution)/shard_map/ppermute | solution.py:339
  92.2 0.2 fusion.5
  92.4 0.1 pad_maximum_fusion.1
  92.5 2.2 %collective-permute-start.8 = (f32[4,128,512]{2,1,0:T(8,128)S(1)}, f32[4,128,512]{2,1,0:T(8,128)S(1)}, u32[]{:S(2)}, u32[]{:S(2)}) collective-permute-start(f32[4,128,512]{2,1,0:T(8,128)S(1)} %pad_maximum_fusion.1), channel_id=1, source_target_pairs={{0,8},{8,16},{16,24},{1,9},{9,17},{17,25},{2,10},{10,18},{18,26},{... | collective-permute-start | bytes 3145736 | tf_op jit(solution)/shard_map/ppermute | solution.py:339
  94.7 12.1 %collective-permute-done.11 = f32[4,128,512]{2,1,0:T(8,128)S(1)} collective-permute-done((f32[4,128,512]{2,1,0:T(8,128)S(1)}, f32[4,128,512]{2,1,0:T(8,128)S(1)}, u32[]{:S(2)}, u32[]{:S(2)}) %collective-permute-start.11) | collective-permute-done | bytes 1048608 | tf_op jit(solution)/shard_map/ppermute | solution.py:340
  106.8 11.0 %collective-permute-done.8 = f32[4,128,512]{2,1,0:T(8,128)S(1)} collective-permute-done((f32[4,128,512]{2,1,0:T(8,128)S(1)}, f32[4,128,512]{2,1,0:T(8,128)S(1)}, u32[]{:S(2)}, u32[]{:S(2)}) %collective-permute-start.8) | collective-permute-done | bytes 1048608 | tf_op jit(solution)/shard_map/ppermute | solution.py:339
  117.8 0.1 fusion.14
  117.9 0.3 fusion.2
  118.2 1.1 pad_maximum_fusion.4
  (3 shorter events, 0.1 us)
Async XLA Ops:
  0.0 15.5 %copy-start = (s32[1,1,16]{2,1,0:T(1,128)S(1)}, s32[1,1,16]{2,1,0:T(1,128)}, u32[]{:S(2)}) copy-start(s32[1,1,16]{2,1,0:T(1,128)} %param.4) | copy-start | bytes 196
  0.0 31.0 %copy-start.1 = (f32[2,4]{1,0:T(2,128)S(1)}, f32[2,4]{1,0:T(2,128)}, u32[]{:S(2)}) copy-start(f32[2,4]{1,0:T(2,128)} %transfer.3) | copy-start | bytes 100
  4.1 26.9 %collective-permute-start.2 = (f32[1536,128]{1,0:T(8,128)}, f32[1536,128]{1,0:T(8,128)S(1)}, u32[]{:S(2)}, u32[]{:S(2)}) collective-permute-start(f32[1536,128]{1,0:T(8,128)} %get-tuple-element.9), channel_id=1, source_target_pairs={{0,8},{8,16},{16,24},{1,9},{9,17},{17,25},{2,10},{10,18},{18,26},{... | collective-permute-start | bytes 2359304 | tf_op jit(solution)/shard_map/ppermute | solution.py:312
  7.7 23.3 %collective-permute-start.3 = (f32[1536,128]{1,0:T(8,128)}, f32[1536,128]{1,0:T(8,128)S(1)}, u32[]{:S(2)}, u32[]{:S(2)}) collective-permute-start(f32[1536,128]{1,0:T(8,128)} %get-tuple-element.10), channel_id=1, source_target_pairs={{8,0},{16,8},{24,16},{9,1},{17,9},{25,17},{10,2},{18,10},{26,18},{... | collective-permute-start | bytes 2359304 | tf_op jit(solution)/shard_map/ppermute | solution.py:313
  10.0 21.0 %collective-permute-start.4 = (f32[16,2048]{1,0:T(8,128)}, f32[16,2048]{1,0:T(8,128)S(1)}, u32[]{:S(2)}, u32[]{:S(2)}) collective-permute-start(f32[16,2048]{1,0:T(8,128)} %get-tuple-element.11), channel_id=1, source_target_pairs={{0,1},{1,2},{2,3},{3,4},{4,5},{5,6},{6,7},{8,9},{9,10},{10,11},{11... | collective-permute-start | bytes 393224 | tf_op jit(solution)/shard_map/ppermute | solution.py:316
  11.9 19.1 %collective-permute-start.5 = (f32[16,2048]{1,0:T(8,128)}, f32[16,2048]{1,0:T(8,128)S(1)}, u32[]{:S(2)}, u32[]{:S(2)}) collective-permute-start(f32[16,2048]{1,0:T(8,128)} %get-tuple-element.12), channel_id=1, source_target_pairs={{1,0},{2,1},{3,2},{4,3},{5,4},{6,5},{7,6},{9,8},{10,9},{11,10},{12... | collective-permute-start | bytes 393224 | tf_op jit(solution)/shard_map/ppermute | solution.py:317
  15.6 10.0 %collective-permute-start = (s32[16]{0:T(128)S(1)}, s32[16]{0:T(128)S(1)}, u32[]{:S(2)}, u32[]{:S(2)}) collective-permute-start(s32[16]{0:T(128)S(1)} %bitcast.33), channel_id=1, source_target_pairs={{0,8},{8,16},{16,24},{1,9},{9,17},{17,25},{2,10},{10,18},{18,26},{... | collective-permute-start | bytes 200 | tf_op jit(solution)/shard_map/ppermute | solution.py:314
  25.5 5.5 %collective-permute-start.1 = (s32[16]{0:T(128)S(1)}, s32[16]{0:T(128)S(1)}, u32[]{:S(2)}, u32[]{:S(2)}) collective-permute-start(s32[16]{0:T(128)S(1)} %bitcast.34), channel_id=1, source_target_pairs={{8,0},{16,8},{24,16},{9,1},{17,9},{25,17},{10,2},{18,10},{26,18},{... | collective-permute-start | bytes 200 | tf_op jit(solution)/shard_map/ppermute | solution.py:315
  35.4 12.4 %collective-permute-start.9 = (f32[4,128,512]{2,1,0:T(8,128)S(1)}, f32[4,128,512]{2,1,0:T(8,128)}, u32[]{:S(2)}, u32[]{:S(2)}) collective-permute-start(f32[4,128,512]{2,1,0:T(8,128)S(1)} %bitcast.30), channel_id=1, source_target_pairs={{24,16},{25,17},{26,18},{27,19},{28,20},{29,21},{30,22},{31,23}} | collective-permute-start | bytes 3145736 | tf_op jit(solution)/shard_map/ppermute | solution.py:340
  37.0 28.5 %collective-permute-start.6 = (f32[4,128,512]{2,1,0:T(8,128)S(1)}, f32[4,128,512]{2,1,0:T(8,128)S(1)}, u32[]{:S(2)}, u32[]{:S(2)}) collective-permute-start(f32[4,128,512]{2,1,0:T(8,128)S(1)} %bitcast.31), channel_id=1, source_target_pairs={{0,8},{1,9},{2,10},{3,11},{4,12},{5,13},{6,14},{7,15}} | collective-permute-start | bytes 3145736 | tf_op jit(solution)/shard_map/ppermute | solution.py:339
  50.2 37.1 %collective-permute-start.10 = (f32[4,128,512]{2,1,0:T(8,128)S(1)}, f32[4,128,512]{2,1,0:T(8,128)S(1)}, u32[]{:S(2)}, u32[]{:S(2)}) collective-permute-start(f32[4,128,512]{2,1,0:T(8,128)S(1)} %pad_maximum_fusion.2), channel_id=1, source_target_pairs={{24,16},{16,8},{25,17},{17,9},{26,18},{18,10},{27,19},{19,11},{28,... | collective-permute-start | bytes 3145736 | tf_op jit(solution)/shard_map/ppermute | solution.py:340
  65.9 26.2 %collective-permute-start.7 = (f32[4,128,512]{2,1,0:T(8,128)S(1)}, f32[4,128,512]{2,1,0:T(8,128)S(1)}, u32[]{:S(2)}, u32[]{:S(2)}) collective-permute-start(f32[4,128,512]{2,1,0:T(8,128)S(1)} %pad_maximum_fusion), channel_id=1, source_target_pairs={{0,8},{8,16},{1,9},{9,17},{2,10},{10,18},{3,11},{11,19},{4,12},{12... | collective-permute-start | bytes 3145736 | tf_op jit(solution)/shard_map/ppermute | solution.py:339
  87.7 19.1 %collective-permute-start.11 = (f32[4,128,512]{2,1,0:T(8,128)S(1)}, f32[4,128,512]{2,1,0:T(8,128)S(1)}, u32[]{:S(2)}, u32[]{:S(2)}) collective-permute-start(f32[4,128,512]{2,1,0:T(8,128)S(1)} %pad_maximum_fusion.3), channel_id=1, source_target_pairs={{24,16},{16,8},{8,0},{25,17},{17,9},{9,1},{26,18},{18,10},{10,2},{... | collective-permute-start | bytes 3145736 | tf_op jit(solution)/shard_map/ppermute | solution.py:340
  92.5 25.4 %collective-permute-start.8 = (f32[4,128,512]{2,1,0:T(8,128)S(1)}, f32[4,128,512]{2,1,0:T(8,128)S(1)}, u32[]{:S(2)}, u32[]{:S(2)}) collective-permute-start(f32[4,128,512]{2,1,0:T(8,128)S(1)} %pad_maximum_fusion.1), channel_id=1, source_target_pairs={{0,8},{8,16},{16,24},{1,9},{9,17},{17,25},{2,10},{10,18},{18,26},{... | collective-permute-start | bytes 3145736 | tf_op jit(solution)/shard_map/ppermute | solution.py:339

commit v2 on v1

v2 whole, which is shorter than its diff:
```python
import functools
import jax
import jax.numpy as jnp
from jax import lax
from jax.experimental import pallas as pl
from jax.experimental.pallas import tpu as pltpu
from jax.sharding import PartitionSpec as P

OCCUPIED_MOST = 12
PAD = 8
ROWS_AT_ONCE = 16
HALVES = 2
LOG2_E = 1.4426950408889634
SMEM = pl.BlockSpec(memory_space=pltpu.SMEM)
VMEM = pl.BlockSpec(memory_space=pltpu.VMEM)
ANY = pl.BlockSpec(memory_space=pl.ANY)
HBM = pl.BlockSpec(memory_space=pltpu.HBM)


def pack_planes_kernel(width, flags, density, head, tail, sem):
    depth_cells, row_cells, _ = density.shape
    block_count = flags.shape[0]
    slots = min(OCCUPIED_MOST, block_count)

    def copies(block, slot):
        columns = pl.ds(pl.multiple_of(block * width, width), width)
        rows = pl.ds(pl.multiple_of(slot * row_cells, row_cells), row_cells)
        return (
            pltpu.make_async_copy(density.at[0, :, columns], head.at[rows, :], sem.at[0, slot]),
            pltpu.make_async_copy(density.at[depth_cells - 1, :, columns], tail.at[rows, :], sem.at[1, slot]),
        )

    def begin(block, slot):
        wanted = jnp.logical_and(flags[block] > 0, slot < slots)

        @pl.when(wanted)
        def _():
            for copy in copies(block, slot):
                copy.start()

        return slot + wanted.astype(jnp.int32)

    used = lax.fori_loop(0, block_count, begin, jnp.int32(0))
    lane = lax.broadcasted_iota(jnp.int32, (8, width), 1)
    row_of_flags = jnp.zeros((8, width), jnp.float32)
    for block in range(block_count):
        row_of_flags = jnp.where(lane == block, flags[block].astype(jnp.float32), row_of_flags)
    head[pl.ds(slots * row_cells, 8), :] = row_of_flags
    tail[pl.ds(slots * row_cells, 8), :] = row_of_flags

    def end(slot, carry):
        for copy in copies(0, slot):
            copy.wait()
        return carry

    lax.fori_loop(0, used, end, 0)


def pack_planes(density, flags, width):
    row_cells = density.shape[1]
    slots = min(OCCUPIED_MOST, flags.shape[0])
    plane = jax.ShapeDtypeStruct((slots * row_cells + 8, width), jnp.float32)
    return pl.pallas_call(
        functools.partial(pack_planes_kernel, width),
        out_shape=(plane, plane),
        in_specs=[SMEM, ANY],
        out_specs=[VMEM] * 2,
        scratch_shapes=[pltpu.SemaphoreType.DMA((2, slots))],
        name="pack_planes",
    )(flags, density)


def pack_rows_kernel(width, flags, density, first_row, last_row, top, bottom, sem):
    depth_cells, row_cells, _ = density.shape
    block_count = flags.shape[0]
    top_copy = pltpu.make_async_copy(density.at[:, 0:8, :], top, sem.at[0])
    bottom_copy = pltpu.make_async_copy(density.at[:, row_cells - 8 : row_cells, :], bottom, sem.at[1])
    top_copy.start()
    bottom_copy.start()
    top_copy.wait()
    bottom_copy.wait()

    def edge(block, carry):
        columns = pl.ds(pl.multiple_of(block * width, width), width)
        flag = flags[block].astype(jnp.float32)
        for z in range(depth_cells):
            first_row[pl.ds(z, 1), columns] = top[z, 0:1, columns] * flag
            last_row[pl.ds(z, 1), columns] = bottom[z, 7:8, columns] * flag
        return carry

    lax.fori_loop(0, block_count, edge, 0)


def pack_rows(density, flags, width):
    depth_cells, _, col_cells = density.shape
    row = jax.ShapeDtypeStruct((depth_cells, col_cells), jnp.float32)
    return pl.pallas_call(
        functools.partial(pack_rows_kernel, width),
        out_shape=(row, row),
        in_specs=[SMEM, ANY],
        out_specs=[VMEM] * 2,
        scratch_shapes=[
            pltpu.VMEM((depth_cells, 8, col_cells), jnp.float32),
            pltpu.VMEM((depth_cells, 8, col_cells), jnp.float32),
            pltpu.SemaphoreType.DMA((2,)),
        ],
        name="pack_rows",
    )(flags, density)


def shade_kernel(
    first_at,
    piece_total,
    width,
    ray_step,
    first_row,
    row_cells,
    flags,
    turned,
    transfer,
    density,
    low_plane,
    high_plane,
    above,
    below,
    *others,
):
    *earlier, out, vol, side_flags, block_sem, plane_sem, flag_sem = others
    depth_cells, all_rows, _ = density.shape
    before = PAD if first_row > 0 else 0
    after = PAD if first_row + row_cells < all_rows else 0
    block_count = flags.shape[0]
    piece_blocks = block_count // piece_total
    skipped = 1 if earlier else 0
    piece_count = out.shape[0] - skipped
    half_rows = out.shape[3]
    slots = min(OCCUPIED_MOST, block_count)
    own = piece_count * piece_blocks
    zero_slot = own + 2
    backward = turned[0] > 0
    first_piece = jnp.where(backward, first_at, piece_total - first_at - piece_count)
    first_block = first_piece * piece_blocks
    body = pl.ds(PAD, row_cells)

    def block_of(slot):
        return first_block + slot - 1

    def occupied(block):
        inside = jnp.logical_and(block >= 0, block < block_count)
        return jnp.logical_and(inside, flags[jnp.clip(block, 0, block_count - 1)] > 0)

    def block_copy(slot):
        block = jnp.clip(block_of(slot), 0, block_count - 1)
        columns = pl.ds(pl.multiple_of(block * width, width), width)
        rows = pl.ds(first_row - before, before + row_cells + after)
        window = pl.ds(PAD - before, before + row_cells + after)
        return pltpu.make_async_copy(
            density.at[:, rows, columns], vol.at[slot, pl.ds(1, depth_cells), window, :], block_sem.at[slot]
        )

    def low_copy(slot, rank):
        rows = pl.ds(pl.multiple_of(rank * all_rows + first_row, row_cells), row_cells)
        return pltpu.make_async_copy(low_plane.at[rows, :], vol.at[slot, 0, body, :], plane_sem.at[0, slot])

    def high_copy(slot, rank):
        rows = pl.ds(pl.multiple_of(rank * all_rows + first_row, row_cells), row_cells)
        return pltpu.make_async_copy(
            high_plane.at[rows, :], vol.at[slot, depth_cells + 1, body, :], plane_sem.at[1, slot]
        )

    def begin_block(slot, carry):
        @pl.when(occupied(block_of(slot)))
        def _():
            block_copy(slot).start()

        return carry

    flag_rows = pl.ds(slots * all_rows, 8)
    flag_copies = [
        pltpu.make_async_copy(plane.at[flag_rows, :], side_flags.at[side], flag_sem.at[side])
        for side, plane in enumerate((low_plane, high_plane))
    ]
    for copy in flag_copies:
        copy.start()
    lax.fori_loop(0, own + 2, begin_block, 0)
    for half, done in enumerate(earlier):
        out[0, half] = done[0, 0]
    for copy in flag_copies:
        copy.wait()

    def begin_plane(block, ranks):
        low_rank, high_rank = ranks
        slot = block - first_block + 1
        mine = jnp.logical_and(jnp.logical_and(slot >= 1, slot <= own), flags[block] > 0)
        low = side_flags[0, 0, block] > 0.5
        high = side_flags[1, 0, block] > 0.5

        @pl.when(jnp.logical_and(mine, low))
        def _():
            low_copy(slot, low_rank).start()

        @pl.when(jnp.logical_and(mine, high))
        def _():
            high_copy(slot, high_rank).start()

        return (low_rank + low.astype(jnp.int32), high_rank + high.astype(jnp.int32))

    lax.fori_loop(0, block_count, begin_plane, (jnp.int32(0), jnp.int32(0)))

    def clear(z, carry):
        vol[zero_slot, z, body, :] = jnp.zeros((row_cells, width), jnp.float32)
        return carry

    lax.fori_loop(1, depth_cells + 1, clear, 0)

    def arrive(slot):
        @pl.when(occupied(block_of(slot)))
        def _():
            block_copy(slot).wait()

    arrive(0)
    arrive(1)

    def visit(slot, carry):
        block = block_of(slot)
        piece = block // piece_blocks - first_piece
        place = skipped + jnp.where(backward, piece, piece_count - 1 - piece)
        columns = pl.ds(pl.multiple_of(lax.rem(block, piece_blocks) * width, width), width)
        arrive(slot + 1)

        @pl.when(jnp.logical_not(occupied(block)))
        def _():
            for half in range(out.shape[1]):
                for channel in range(4):
                    value = 1.0 if channel == 3 else 0.0
                    out[place, half, channel, :, columns] = jnp.full((half_rows, width), value, jnp.float32)

        @pl.when(occupied(block))
        def _():
            left = jnp.where(occupied(block - 1), slot - 1, zero_slot)
            right = jnp.where(occupied(block + 1), slot + 1, zero_slot)
            source = pl.ds(pl.multiple_of(block * width, width), width)
            for z in range(depth_cells):
                if not before:
                    vol[slot, z + 1, pl.ds(PAD - 1, 1), :] = above[pl.ds(z, 1), source]
                if not after:
                    vol[slot, z + 1, pl.ds(PAD + row_cells, 1), :] = below[pl.ds(z, 1), source]
            for side, plane_copy in enumerate((low_copy, high_copy)):
                near = side_flags[side, 0, block] > 0.5

                @pl.when(near)
                def _():
                    plane_copy(slot, 0).wait()

                @pl.when(jnp.logical_not(near))
                def _():
                    vol[slot, side * (depth_cells + 1), body, :] = jnp.zeros((row_cells, width), jnp.float32)

            march(slot, left, right, place, columns)

        return carry

    def march(slot, left, right, place, columns):
        rows_at_once = ROWS_AT_ONCE
        shape = (rows_at_once, width)
        lane = lax.broadcasted_iota(jnp.int32, shape, 1)
        at_first = lane == 0
        at_last = lane == width - 1
        slopes = [transfer[0, channel] * 0.5 for channel in range(3)]
        offsets = [transfer[1, channel] * 0.5 for channel in range(3)]
        decay_slope = transfer[0, 3] * LOG2_E
        decay_offset = transfer[1, 3] * LOG2_E

        def chunk(at, carry):
            start = pl.multiple_of(PAD + at * rows_at_once, 8)
            rows = pl.ds(start, rows_at_once)
            previous = vol[slot, 0, rows, :]
            center = vol[slot, 1, rows, :]
            transmit = jnp.ones(shape, jnp.float32)
            plain = jnp.zeros(shape, jnp.float32)
            tinted = [jnp.zeros(shape, jnp.float32) for _ in range(3)]
            for z in range(1, depth_cells + 1):
                following = vol[slot, z + 1, rows, :]
                diff_z = following - previous
                diff_y = vol[slot, z, pl.ds(start + 1, rows_at_once), :] - vol[slot, z, pl.ds(start - 1, rows_at_once), :]
                right_side = pltpu.roll(jnp.where(at_first, vol[right, z, rows, :], center), width - 1, 1)
                left_side = pltpu.roll(jnp.where(at_last, vol[left, z, rows, :], center), 1, 1)
                diff_x = right_side - left_side
                facing = jnp.abs(diff_x + 0.9375 * diff_y + 0.75 * diff_z)
                norm = lax.rsqrt(diff_x * diff_x + diff_y * diff_y + (diff_z * diff_z + 4.0))
                lighting = facing * norm + (0.3 / 0.448)
                soft = jnp.log(1.0 + jnp.exp2(decay_slope * center + decay_offset))
                passed = transmit * jnp.exp2((center * (-ray_step * LOG2_E)) * soft)
                weight = (transmit - passed) * lighting
                transmit = passed
                plain = plain + weight
                for channel in range(3):
                    tinted[channel] = tinted[channel] + weight * jnp.tanh(slopes[channel] * center + offsets[channel])
                previous, center = center, following
            half = at // (half_rows // rows_at_once)
            target = pl.ds(pl.multiple_of(at * rows_at_once - half * half_rows, 8), rows_at_once)
            for channel in range(3):
                out[place, half, channel, target, columns] = 0.224 * (plain + tinted[channel])
            out[place, half, 3, target, columns] = transmit
            return carry

        lax.fori_loop(0, row_cells // rows_at_once, chunk, 0)

    lax.fori_loop(1, own + 1, visit, 0)


def shade(first_at, piece_count, piece_total, ray_step, first_row, rows, halves, flags, turned, transfer, density, low_plane, high_plane, above, below, *earlier):
    depth_cells, _, col_cells = density.shape
    block_count = flags.shape[0]
    width = col_cells // block_count
    own = piece_count * (block_count // piece_total)
    cells = own * depth_cells * rows * width
    shape = (piece_count + (1 if earlier else 0), halves, 4, rows // halves, col_cells // piece_total)
    return pl.pallas_call(
        functools.partial(shade_kernel, first_at, piece_total, width, ray_step, first_row, rows),
        out_shape=jax.ShapeDtypeStruct(shape, jnp.float32),
        in_specs=[SMEM] * 3 + [ANY] * 3 + [VMEM] * (2 + len(earlier)),
        out_specs=VMEM,
        scratch_shapes=[
            pltpu.VMEM((own + 3, depth_cells + 2, rows + 2 * PAD, width), jnp.float32),
            pltpu.SMEM((2, 8, width), jnp.float32),
            pltpu.SemaphoreType.DMA((own + 2,)),
            pltpu.SemaphoreType.DMA((2, own + 2)),
            pltpu.SemaphoreType.DMA((2,)),
        ],
        compiler_params=pltpu.CompilerParams(vmem_limit_bytes=48 << 20),
        cost_estimate=pl.CostEstimate(flops=60 * cells, bytes_accessed=4 * cells, transcendentals=7 * cells),
        name=f"shade_{first_at}_{first_row}",
    )(flags, turned, transfer, density, low_plane, high_plane, above, below, *earlier)


def merge_kernel(half, table, pieces, front, back, up, down, own, sem):
    copies = [pltpu.make_async_copy(pieces.at[table[side], half], own.at[side], sem.at[side]) for side in range(2)]
    for copy in copies:
        copy.start()
    opening = jnp.where(table[2] > 0, front[3], 1.0)
    closing = jnp.where(table[3] > 0, back[3], 1.0)
    copies[0].wait()
    up[3] = opening * own[0, 3]
    for channel in range(3):
        up[channel] = front[channel] + opening * own[0, channel]
    copies[1].wait()
    passed = own[1, 3]
    down[3] = passed * closing
    for channel in range(3):
        down[channel] = own[1, channel] + passed * back[channel]


def merge(half, table, pieces, front, back):
    part = pieces.shape[2:]
    cells = part[0] * part[1] * part[2]
    return pl.pallas_call(
        functools.partial(merge_kernel, half),
        out_shape=(jax.ShapeDtypeStruct(part, jnp.float32),) * 2,
        in_specs=[SMEM, HBM, VMEM, VMEM],
        out_specs=[VMEM, VMEM],
        scratch_shapes=[pltpu.VMEM((2,) + part, jnp.float32), pltpu.SemaphoreType.DMA((2,))],
        compiler_params=pltpu.CompilerParams(vmem_limit_bytes=16 << 20),
        cost_estimate=pl.CostEstimate(flops=4 * cells, bytes_accessed=24 * cells, transcendentals=0),
        name="merge",
    )(table, pieces, front, back)


def finish_kernel(half, table, pieces, front, back, *others):
    image, own, made, sem = others[-4:]
    rows = pl.ds(half * made.shape[1], made.shape[1])
    load = pltpu.make_async_copy(pieces.at[table[0], half], own, sem.at[0])
    load.start()
    opening = jnp.where(table[2] > 0, front[3], 1.0)
    closing = jnp.where(table[3] > 0, back[3], 1.0)
    load.wait()
    passed = opening * own[3]
    for channel in range(3):
        made[channel] = front[channel] + opening * own[channel] + passed * back[channel]
    made[3] = 1.0 - passed * closing
    store = pltpu.make_async_copy(made, image.at[:, rows, :], sem.at[1])
    store.start()
    store.wait()


def finish(half, table, pieces, front, back, image):
    part = pieces.shape[2:]
    cells = part[0] * part[1] * part[2]
    started = [] if image is None else [image]
    return pl.pallas_call(
        functools.partial(finish_kernel, half),
        out_shape=jax.ShapeDtypeStruct((part[0], HALVES * part[1], part[2]), jnp.float32),
        in_specs=[SMEM, HBM, VMEM, VMEM] + [ANY] * len(started),
        out_specs=ANY,
        scratch_shapes=[pltpu.VMEM(part, jnp.float32), pltpu.VMEM(part, jnp.float32), pltpu.SemaphoreType.DMA((2,))],
        input_output_aliases={4: 0} if started else {},
        compiler_params=pltpu.CompilerParams(vmem_limit_bytes=16 << 20),
        cost_estimate=pl.CostEstimate(flops=4 * cells, bytes_accessed=16 * cells, transcendentals=0),
        name="finish",
    )(table, pieces, front, back, *started)


def shards(density, occupancy, transfer):
    depth_cells, row_cells, col_cells = density.shape
    flags = occupancy.reshape(-1)
    block_count = flags.shape[0]
    width = col_cells // block_count
    count = lax.axis_size("depth")
    slabs = lax.axis_size("rows")
    position = lax.axis_index("depth")
    ray_step = 2.0 / (depth_cells * count)
    later = [(i, i + 1) for i in range(count - 1)]
    sooner = [(i + 1, i) for i in range(count - 1)]

    head, tail = pack_planes(density, flags, width)
    low_plane = lax.ppermute(tail, "depth", later)
    high_plane = lax.ppermute(head, "depth", sooner)
    first_row, last_row = pack_rows(density, flags, width)
    above = lax.ppermute(last_row, "rows", [(i, i + 1) for i in range(slabs - 1)])
    below = lax.ppermute(first_row, "rows", [(i + 1, i) for i in range(slabs - 1)])
    backward = position >= count // 2
    turned = backward.astype(jnp.int32).reshape(1)
    args = (flags, turned, transfer, density, low_plane, high_plane, above, below)
    half_rows = row_cells // HALVES
    first = [shade(0, 1, count, ray_step, half * half_rows, half_rows, 1, *args) for half in range(HALVES)]
    pieces = shade(1, count - 1, count, ray_step, 0, row_cells, HALVES, *args, *first)

    def place(piece):
        return jnp.clip(jnp.where(backward, piece, count - 1 - piece), 0, count - 1)

    def table(up_piece, down_piece):
        sides = [position > 0, position < count - 1]
        return jnp.stack([place(up_piece), place(down_piece)] + [side.astype(jnp.int32) for side in sides])

    fronts, backs = [None] * HALVES, [None] * HALVES
    for step in range(count - 1):
        ups = [(i, i + 1) for i in range(step + 1)]
        downs = [(count - 1 - i, count - 2 - i) for i in range(step + 1)]
        apart = step + 1 < count - 2 - step
        step_table = table(count - 1 - step + position, step + position - (count - 1))
        for half in range(HALVES):
            if step:
                up, down = merge(half, step_table, pieces, fronts[half], backs[half])
            else:
                up = down = first[half][0, 0]
            if apart:
                sent = jnp.where(backward, down, up) if step else up
                fronts[half] = backs[half] = lax.ppermute(sent, "depth", ups + downs)
            else:
                fronts[half] = lax.ppermute(up, "depth", ups)
                backs[half] = lax.ppermute(down, "depth", downs)
    image = None
    final_table = table(position, position)
    for half in range(HALVES):
        image = finish(half, final_table, pieces, fronts[half], backs[half], image)
    return image


def solution(mesh):
    in_specs = (P("depth", "rows", None), P("depth", "rows", None), P())
    out_specs = P(None, "rows", "depth")
    return jax.shard_map(shards, mesh=mesh, in_specs=in_specs, out_specs=out_specs, check_vma=False)
```

time: 122 us -> 120 us (0.984)
  the two profiles are of different devices: /device:TPU:10 before, /device:TPU:0 now
where the time goes in v2:
time: 120 us; the launch traced here: 121 us
  starting transfers between devices  42.4 us (35%)
  Pallas kernels  39.2 us (33%)
  waiting for transfers between devices  32.2 us (27%)
  local copies, waits for them, and re-layouts  6.56 us (5%)
    ppermute x4, starting transfers between devices, shards(): fronts[half] = lax.ppermute(up, 'depth', ups)  24.4 us
    pallas_call x3, Pallas kernels, shade(): pl.pallas_call(functools.partial(shade_kernel, first_at, piece_total, wid...  24.1 us
    ppermute x4, waiting for transfers between devices, shards(): backs[half] = lax.ppermute(down, 'depth', downs)  13.7 us
    unnamed x10, local copies, waits for them, and re-layouts  6.56 us
    ppermute x1, waiting for transfers between devices, shards(): low_plane = lax.ppermute(tail, 'depth', later)  6.14 us
    pallas_call x4, Pallas kernels, merge(): pl.pallas_call(functools.partial(merge_kernel, half), out_shape=(jax.Shap...  5.51 us
    ppermute x1, starting transfers between devices, shards(): low_plane = lax.ppermute(tail, 'depth', later)  5.05 us
    ppermute x2, starting transfers between devices, shards(): fronts[half] = backs[half] = lax.ppermute(sent, 'depth', ups + downs)  4.79 us
  transfers between devices with their start and end apart: 14, of which 8 were waited for; matrix products, arithmetic and copies ran while one was open for 0% of the time, Pallas kernels for 24%

profile of v2, /device:TPU:0, one launch (start us, length us, event | category | flops | bytes accessed | tf_op | source)
XLA Modules:
  0.0 120.8 jit_solution(17396904268656838884)
XLA Ops:
  0.0 3.4 %pack_planes.1 = (f32[1544,128]{1,0:T(8,128)}, f32[1544,128]{1,0:T(8,128)}) custom-call(s32[16]{0:T(128)} %bitcast.12, f32[16,128,2048]{2,1,0:T(8,128)} %density.9), custom_call_target="tpu_custom_call" | custom-call | tf_op jit(solution)/shard_map/pack_planes/pallas_call | solution.py:63
  3.4 5.0 %collective-permute-start = (f32[1544,128]{1,0:T(8,128)}, f32[1544,128]{1,0:T(8,128)S(1)}, u32[]{:S(2)}, u32[]{:S(2)}) collective-permute-start(f32[1544,128]{1,0:T(8,128)} %get-tuple-element.17), channel_id=1, source_target_pairs={{0,8},{8,16},{16,24},{1,9},{9,17},{17,25},{2,10},{10,18},{18,26},{... | collective-permute-start | bytes 2371592 | tf_op jit(solution)/shard_map/ppermute | solution.py:416
  8.5 1.3 %collective-permute-start.1 = (f32[1544,128]{1,0:T(8,128)}, f32[1544,128]{1,0:T(8,128)S(1)}, u32[]{:S(2)}, u32[]{:S(2)}) collective-permute-start(f32[1544,128]{1,0:T(8,128)} %get-tuple-element.18), channel_id=1, source_target_pairs={{8,0},{16,8},{24,16},{9,1},{17,9},{25,17},{10,2},{18,10},{26,18},{... | collective-permute-start | bytes 2371592 | tf_op jit(solution)/shard_map/ppermute | solution.py:417
  9.8 3.2 %pack_rows.1 = (f32[16,2048]{1,0:T(8,128)}, f32[16,2048]{1,0:T(8,128)}) custom-call(s32[16]{0:T(128)} %bitcast.13, f32[16,128,2048]{2,1,0:T(8,128)} %density.9), custom_call_target="tpu_custom_call" | custom-call | tf_op jit(solution)/shard_map/pack_rows/pallas_call | solution.py:97
  13.0 1.5 %collective-permute-start.2 = (f32[16,2048]{1,0:T(8,128)}, f32[16,2048]{1,0:T(8,128)S(1)}, u32[]{:S(2)}, u32[]{:S(2)}) collective-permute-start(f32[16,2048]{1,0:T(8,128)} %get-tuple-element.19), channel_id=1, source_target_pairs={{0,1},{1,2},{2,3},{3,4},{4,5},{5,6},{6,7},{8,9},{9,10},{10,11},{11... | collective-permute-start | bytes 393224 | tf_op jit(solution)/shard_map/ppermute | solution.py:419
  14.5 1.3 %collective-permute-start.3 = (f32[16,2048]{1,0:T(8,128)}, f32[16,2048]{1,0:T(8,128)S(1)}, u32[]{:S(2)}, u32[]{:S(2)}) collective-permute-start(f32[16,2048]{1,0:T(8,128)} %get-tuple-element.20), channel_id=1, source_target_pairs={{1,0},{2,1},{3,2},{4,3},{5,4},{6,5},{7,6},{9,8},{10,9},{11,10},{12... | collective-permute-start | bytes 393224 | tf_op jit(solution)/shard_map/ppermute | solution.py:420
  15.8 0.0 collective-permute-done.2.above
  15.8 3.7 %collective-permute-done.3.below = f32[16,2048]{1,0:T(8,128)S(1)} collective-permute-done((f32[16,2048]{1,0:T(8,128)}, f32[16,2048]{1,0:T(8,128)S(1)}, u32[]{:S(2)}, u32[]{:S(2)}) %collective-permute-start.3) | collective-permute-done | bytes 131104 | tf_op jit(solution)/shard_map/ppermute | solution.py:420
  19.5 6.1 %collective-permute-done.low_plane = f32[1544,128]{1,0:T(8,128)S(1)} collective-permute-done((f32[1544,128]{1,0:T(8,128)}, f32[1544,128]{1,0:T(8,128)S(1)}, u32[]{:S(2)}, u32[]{:S(2)}) %collective-permute-start) | collective-permute-done | bytes 790560 | tf_op jit(solution)/shard_map/ppermute | solution.py:416
  25.7 4.1 %collective-permute-done.1.high_plane = f32[1544,128]{1,0:T(8,128)S(1)} collective-permute-done((f32[1544,128]{1,0:T(8,128)}, f32[1544,128]{1,0:T(8,128)S(1)}, u32[]{:S(2)}, u32[]{:S(2)}) %collective-permute-start.1) | collective-permute-done | bytes 790560 | tf_op jit(solution)/shard_map/ppermute | solution.py:417
  29.7 0.0 copy-done.3
  29.7 0.0 copy-done.4
  29.7 5.0 %shade_0_0.1.others_0_ = f32[1,1,4,64,512]{4,3,2,1,0:T(8,128)} custom-call(s32[16]{0:T(128)S(1)} %bitcast.14, s32[1]{0:T(128)} %bitcast.4.turned, f32[2,4]{1,0:T(2,128)S(1)} %copy-done.4, f32[16,128,2048]{2,1,0:T(8,128)} %density.9, f32[1544,128]{1,0:T(8,128)S(1)} %collective-permute-done.low_plane, f32[1544,128]{1,0:T(8,128)S(1)} %collective-permute-done.1.high_plane, ...), custom_call_target="tpu_custom_call" | custom-call | flops 31457280 | bytes 2097152 | tf_op jit(solution)/shard_map/shade_0_0/pallas_call | solution.py:319
  34.8 3.5 %collective-permute-start.9 = (f32[4,64,512]{2,1,0:T(8,128)}, f32[4,64,512]{2,1,0:T(8,128)S(1)}, u32[]{:S(2)}, u32[]{:S(2)}) collective-permute-start(f32[4,64,512]{2,1,0:T(8,128)} %bitcast.10), channel_id=1, source_target_pairs={{0,8},{24,16},{1,9},{25,17},{2,10},{26,18},{3,11},{27,19},{4,12},{... | collective-permute-start | bytes 1572872 | tf_op jit(solution)/shard_map/ppermute | solution.py:448
  38.2 4.2 %shade_0_64.1.others_1_ = f32[1,1,4,64,512]{4,3,2,1,0:T(8,128)S(1)} custom-call(s32[16]{0:T(128)S(1)} %bitcast.15, s32[1]{0:T(128)} %bitcast.4.turned, f32[2,4]{1,0:T(2,128)S(1)} %copy-done.4, f32[16,128,2048]{2,1,0:T(8,128)} %density.9, f32[1544,128]{1,0:T(8,128)S(1)} %collective-permute-done.low_plane, f32[1544,128]{1,0:T(8,128)S(1)} %collective-permute-done.1.high_plane, ...), custom_call_target="tpu_custom_call" | custom-call | flops 31457280 | bytes 2097152 | tf_op jit(solution)/shard_map/shade_0_64/pallas_call | solution.py:319
  42.5 1.3 %collective-permute-start.4 = (f32[4,64,512]{2,1,0:T(8,128)S(1)}, f32[4,64,512]{2,1,0:T(8,128)S(1)}, u32[]{:S(2)}, u32[]{:S(2)}) collective-permute-start(f32[4,64,512]{2,1,0:T(8,128)S(1)} %bitcast.11), channel_id=1, source_target_pairs={{0,8},{24,16},{1,9},{25,17},{2,10},{26,18},{3,11},{27,19},{4,12},{... | collective-permute-start | bytes 1572872 | tf_op jit(solution)/shard_map/ppermute | solution.py:448
  43.8 0.1 add_add_fusion.2.table
  43.9 14.8 %shade_1_0.1.pieces = f32[4,2,4,64,512]{4,3,2,1,0:T(8,128)} custom-call(s32[16]{0:T(128)S(1)} %bitcast.16, s32[1]{0:T(128)} %bitcast.4.turned, f32[2,4]{1,0:T(2,128)S(1)} %copy-done.4, f32[16,128,2048]{2,1,0:T(8,128)} %density.9, f32[1544,128]{1,0:T(8,128)S(1)} %collective-permute-done.low_plane, f32[1544,128]{1,0:T(8,128)S(1)} %collective-permute-done.1.high_plane, ...), custom_call_target="tpu_custom_call" | custom-call | flops 188743680 | bytes 12582912 | tf_op jit(solution)/shard_map/shade_1_0/pallas_call | solution.py:319
  58.8 0.0 collective-permute-done.9.front.back
  58.8 0.0 copy-start
  58.8 2.2 %copy-done = f32[4,2,4,64,512]{4,3,2,1,0:T(8,128)S(1)} copy-done((f32[4,2,4,64,512]{4,3,2,1,0:T(8,128)S(1)}, f32[4,2,4,64,512]{4,3,2,1,0:T(8,128)}, u32[]{:S(2)}) %copy-start) | copy-done | bytes 4194328
  61.0 1.5 %merge.6 = (f32[4,64,512]{2,1,0:T(8,128)}, f32[4,64,512]{2,1,0:T(8,128)S(1)}) custom-call(s32[4]{0:T(128)S(1)} %add_add_fusion.2.table, f32[4,2,4,64,512]{4,3,2,1,0:T(8,128)S(1)} %copy-done, f32[4,64,512]{2,1,0:T(8,128)S(1)} %collective-permute-done.9.front.back, f32[4,64,512]{2,1,0:T(8,128)S(1)} %collective-permute-done.9.front.back), custom_call_target="tpu_custom_call" | custom-call | flops 524288 | bytes 3145728 | tf_op jit(solution)/shard_map/merge/pallas_call | solution.py:357
  62.5 3.3 %collective-permute-start.10 = (f32[4,64,512]{2,1,0:T(8,128)}, f32[4,64,512]{2,1,0:T(8,128)S(1)}, u32[]{:S(2)}, u32[]{:S(2)}) collective-permute-start(f32[4,64,512]{2,1,0:T(8,128)} %get-tuple-element.25), channel_id=1, source_target_pairs={{0,8},{8,16},{1,9},{9,17},{2,10},{10,18},{3,11},{11,19},{4,12},{12... | collective-permute-start | bytes 1572872 | tf_op jit(solution)/shard_map/ppermute | solution.py:450
  65.7 0.7 collective-permute-start.11
  66.4 0.0 collective-permute-done.4.front.back
  66.5 1.5 %merge.4 = (f32[4,64,512]{2,1,0:T(8,128)}, f32[4,64,512]{2,1,0:T(8,128)S(1)}) custom-call(s32[4]{0:T(128)S(1)} %add_add_fusion.2.table, f32[4,2,4,64,512]{4,3,2,1,0:T(8,128)S(1)} %copy-done, f32[4,64,512]{2,1,0:T(8,128)S(1)} %collective-permute-done.4.front.back, f32[4,64,512]{2,1,0:T(8,128)S(1)} %collective-permute-done.4.front.back), custom_call_target="tpu_custom_call" | custom-call | flops 524288 | bytes 3145728 | tf_op jit(solution)/shard_map/merge/pallas_call | solution.py:357
  68.0 5.5 %collective-permute-start.5 = (f32[4,64,512]{2,1,0:T(8,128)}, f32[4,64,512]{2,1,0:T(8,128)S(1)}, u32[]{:S(2)}, u32[]{:S(2)}) collective-permute-start(f32[4,64,512]{2,1,0:T(8,128)} %get-tuple-element.21), channel_id=1, source_target_pairs={{0,8},{8,16},{1,9},{9,17},{2,10},{10,18},{3,11},{11,19},{4,12},{12... | collective-permute-start | bytes 1572872 | tf_op jit(solution)/shard_map/ppermute | solution.py:450
  73.5 0.7 collective-permute-start.6
  74.2 0.1 add_add_fusion.1.table
  74.3 2.4 %collective-permute-done.10.front = f32[4,64,512]{2,1,0:T(8,128)S(1)} collective-permute-done((f32[4,64,512]{2,1,0:T(8,128)}, f32[4,64,512]{2,1,0:T(8,128)S(1)}, u32[]{:S(2)}, u32[]{:S(2)}) %collective-permute-start.10) | collective-permute-done | bytes 524320 | tf_op jit(solution)/shard_map/ppermute | solution.py:450
  76.7 0.0 collective-permute-done.11.back
  76.7 2.2 %copy-done.1 = f32[4,2,4,64,512]{4,3,2,1,0:T(8,128)S(1)} copy-done((f32[4,2,4,64,512]{4,3,2,1,0:T(8,128)S(1)}, f32[4,2,4,64,512]{4,3,2,1,0:T(8,128)}, u32[]{:S(2)}) %copy-start.1) | copy-done | bytes 4194328
  78.9 1.7 %merge.7 = (f32[4,64,512]{2,1,0:T(8,128)}, f32[4,64,512]{2,1,0:T(8,128)}) custom-call(s32[4]{0:T(128)S(1)} %add_add_fusion.1.table, f32[4,2,4,64,512]{4,3,2,1,0:T(8,128)S(1)} %copy-done.1, f32[4,64,512]{2,1,0:T(8,128)S(1)} %collective-permute-done.10.front, f32[4,64,512]{2,1,0:T(8,128)S(1)} %collective-permute-done.11.back), custom_call_target="tpu_custom_call" | custom-call | flops 524288 | bytes 3145728 | tf_op jit(solution)/shard_map/merge/pallas_call | solution.py:357
  80.6 9.6 %collective-permute-start.12 = (f32[4,64,512]{2,1,0:T(8,128)}, f32[4,64,512]{2,1,0:T(8,128)S(1)}, u32[]{:S(2)}, u32[]{:S(2)}) collective-permute-start(f32[4,64,512]{2,1,0:T(8,128)} %get-tuple-element.27), channel_id=1, source_target_pairs={{0,8},{8,16},{16,24},{1,9},{9,17},{17,25},{2,10},{10,18},{18,26},{... | collective-permute-start | bytes 1572872 | tf_op jit(solution)/shard_map/ppermute | solution.py:450
  90.2 1.3 %collective-permute-start.13 = (f32[4,64,512]{2,1,0:T(8,128)}, f32[4,64,512]{2,1,0:T(8,128)S(1)}, u32[]{:S(2)}, u32[]{:S(2)}) collective-permute-start(f32[4,64,512]{2,1,0:T(8,128)} %get-tuple-element.28), channel_id=1, source_target_pairs={{24,16},{16,8},{8,0},{25,17},{17,9},{9,1},{26,18},{18,10},{10,2},{... | collective-permute-start | bytes 1572872 | tf_op jit(solution)/shard_map/ppermute | solution.py:451
  91.5 0.0 collective-permute-done.5.front
  91.5 0.0 collective-permute-done.6.back
  91.6 0.8 merge.5
  92.3 6.0 %collective-permute-start.7 = (f32[4,64,512]{2,1,0:T(8,128)S(1)}, f32[4,64,512]{2,1,0:T(8,128)S(1)}, u32[]{:S(2)}, u32[]{:S(2)}) collective-permute-start(f32[4,64,512]{2,1,0:T(8,128)S(1)} %get-tuple-element.23), channel_id=1, source_target_pairs={{0,8},{8,16},{16,24},{1,9},{9,17},{17,25},{2,10},{10,18},{18,26},{... | collective-permute-start | bytes 1572872 | tf_op jit(solution)/shard_map/ppermute | solution.py:450
  98.4 1.3 %collective-permute-start.8 = (f32[4,64,512]{2,1,0:T(8,128)S(1)}, f32[4,64,512]{2,1,0:T(8,128)S(1)}, u32[]{:S(2)}, u32[]{:S(2)}) collective-permute-start(f32[4,64,512]{2,1,0:T(8,128)S(1)} %get-tuple-element.24), channel_id=1, source_target_pairs={{24,16},{16,8},{8,0},{25,17},{17,9},{9,1},{26,18},{18,10},{10,2},{... | collective-permute-start | bytes 1572872 | tf_op jit(solution)/shard_map/ppermute | solution.py:451
  99.7 0.1 add_add_fusion.table
  99.7 1.8 %collective-permute-done.12.front = f32[4,64,512]{2,1,0:T(8,128)S(1)} collective-permute-done((f32[4,64,512]{2,1,0:T(8,128)}, f32[4,64,512]{2,1,0:T(8,128)S(1)}, u32[]{:S(2)}, u32[]{:S(2)}) %collective-permute-start.12) | collective-permute-done | bytes 524320 | tf_op jit(solution)/shard_map/ppermute | solution.py:450
  101.6 7.0 %collective-permute-done.13.back = f32[4,64,512]{2,1,0:T(8,128)S(1)} collective-permute-done((f32[4,64,512]{2,1,0:T(8,128)}, f32[4,64,512]{2,1,0:T(8,128)S(1)}, u32[]{:S(2)}, u32[]{:S(2)}) %collective-permute-start.13) | collective-permute-done | bytes 524320 | tf_op jit(solution)/shard_map/ppermute | solution.py:451
  108.6 2.2 %copy-done.2 = f32[4,2,4,64,512]{4,3,2,1,0:T(8,128)S(1)} copy-done((f32[4,2,4,64,512]{4,3,2,1,0:T(8,128)S(1)}, f32[4,2,4,64,512]{4,3,2,1,0:T(8,128)}, u32[]{:S(2)}) %copy-start.2) | copy-done | bytes 4194328
  110.8 1.5 %finish.2.others_0_ = f32[4,128,512]{2,1,0:T(8,128)} custom-call(s32[4]{0:T(128)S(1)} %add_add_fusion.table, f32[4,2,4,64,512]{4,3,2,1,0:T(8,128)S(1)} %copy-done.2, f32[4,64,512]{2,1,0:T(8,128)S(1)} %collective-permute-done.12.front, f32[4,64,512]{2,1,0:T(8,128)S(1)} %collective-permute-done.13.back), custom_call_target="tpu_custom_call" | custom-call | flops 524288 | bytes 2097152 | tf_op jit(solution)/shard_map/finish/pallas_call | solution.py:390
  112.3 0.4 collective-permute-done.7.front
  112.7 6.6 %collective-permute-done.8.back = f32[4,64,512]{2,1,0:T(8,128)S(1)} collective-permute-done((f32[4,64,512]{2,1,0:T(8,128)S(1)}, f32[4,64,512]{2,1,0:T(8,128)S(1)}, u32[]{:S(2)}, u32[]{:S(2)}) %collective-permute-start.8) | collective-permute-done | bytes 524320 | tf_op jit(solution)/shard_map/ppermute | solution.py:451
  119.3 1.5 %finish.3 = f32[4,128,512]{2,1,0:T(8,128)} custom-call(s32[4]{0:T(128)S(1)} %add_add_fusion.table, f32[4,2,4,64,512]{4,3,2,1,0:T(8,128)S(1)} %copy-done.2, f32[4,64,512]{2,1,0:T(8,128)S(1)} %collective-permute-done.7.front, f32[4,64,512]{2,1,0:T(8,128)S(1)} %collective-permute-done.8.back, ...), custom_call_target="tpu_custom_call", output_to_operand_aliasing={{}: (4, {})} | custom-call | flops 524288 | bytes 2097152 | tf_op jit(solution)/shard_map/finish/pallas_call | solution.py:390
  (4 shorter events, 0.0 us)
Async XLA Ops:
  0.0 29.7 %copy-start.3 = (s32[1,1,16]{2,1,0:T(1,128)S(1)}, s32[1,1,16]{2,1,0:T(1,128)}, u32[]{:S(2)}) copy-start(s32[1,1,16]{2,1,0:T(1,128)} %param.4) | copy-start | bytes 196
  0.0 29.7 %copy-start.4 = (f32[2,4]{1,0:T(2,128)S(1)}, f32[2,4]{1,0:T(2,128)}, u32[]{:S(2)}) copy-start(f32[2,4]{1,0:T(2,128)} %transfer.5) | copy-start | bytes 100
  3.4 22.3 %collective-permute-start = (f32[1544,128]{1,0:T(8,128)}, f32[1544,128]{1,0:T(8,128)S(1)}, u32[]{:S(2)}, u32[]{:S(2)}) collective-permute-start(f32[1544,128]{1,0:T(8,128)} %get-tuple-element.17), channel_id=1, source_target_pairs={{0,8},{8,16},{16,24},{1,9},{9,17},{17,25},{2,10},{10,18},{18,26},{... | collective-permute-start | bytes 2371592 | tf_op jit(solution)/shard_map/ppermute | solution.py:416
  8.5 21.3 %collective-permute-start.1 = (f32[1544,128]{1,0:T(8,128)}, f32[1544,128]{1,0:T(8,128)S(1)}, u32[]{:S(2)}, u32[]{:S(2)}) collective-permute-start(f32[1544,128]{1,0:T(8,128)} %get-tuple-element.18), channel_id=1, source_target_pairs={{8,0},{16,8},{24,16},{9,1},{17,9},{25,17},{10,2},{18,10},{26,18},{... | collective-permute-start | bytes 2371592 | tf_op jit(solution)/shard_map/ppermute | solution.py:417
  13.0 2.9 %collective-permute-start.2 = (f32[16,2048]{1,0:T(8,128)}, f32[16,2048]{1,0:T(8,128)S(1)}, u32[]{:S(2)}, u32[]{:S(2)}) collective-permute-start(f32[16,2048]{1,0:T(8,128)} %get-tuple-element.19), channel_id=1, source_target_pairs={{0,1},{1,2},{2,3},{3,4},{4,5},{5,6},{6,7},{8,9},{9,10},{10,11},{11... | collective-permute-start | bytes 393224 | tf_op jit(solution)/shard_map/ppermute | solution.py:419
  14.5 5.0 %collective-permute-start.3 = (f32[16,2048]{1,0:T(8,128)}, f32[16,2048]{1,0:T(8,128)S(1)}, u32[]{:S(2)}, u32[]{:S(2)}) collective-permute-start(f32[16,2048]{1,0:T(8,128)} %get-tuple-element.20), channel_id=1, source_target_pairs={{1,0},{2,1},{3,2},{4,3},{5,4},{6,5},{7,6},{9,8},{10,9},{11,10},{12... | collective-permute-start | bytes 393224 | tf_op jit(solution)/shard_map/ppermute | solution.py:420
  34.8 24.0 %collective-permute-start.9 = (f32[4,64,512]{2,1,0:T(8,128)}, f32[4,64,512]{2,1,0:T(8,128)S(1)}, u32[]{:S(2)}, u32[]{:S(2)}) collective-permute-start(f32[4,64,512]{2,1,0:T(8,128)} %bitcast.10), channel_id=1, source_target_pairs={{0,8},{24,16},{1,9},{25,17},{2,10},{26,18},{3,11},{27,19},{4,12},{... | collective-permute-start | bytes 1572872 | tf_op jit(solution)/shard_map/ppermute | solution.py:448
  42.5 24.0 %collective-permute-start.4 = (f32[4,64,512]{2,1,0:T(8,128)S(1)}, f32[4,64,512]{2,1,0:T(8,128)S(1)}, u32[]{:S(2)}, u32[]{:S(2)}) collective-permute-start(f32[4,64,512]{2,1,0:T(8,128)S(1)} %bitcast.11), channel_id=1, source_target_pairs={{0,8},{24,16},{1,9},{25,17},{2,10},{26,18},{3,11},{27,19},{4,12},{... | collective-permute-start | bytes 1572872 | tf_op jit(solution)/shard_map/ppermute | solution.py:448
  58.8 2.2 %copy-start = (f32[4,2,4,64,512]{4,3,2,1,0:T(8,128)S(1)}, f32[4,2,4,64,512]{4,3,2,1,0:T(8,128)}, u32[]{:S(2)}) copy-start(f32[4,2,4,64,512]{4,3,2,1,0:T(8,128)} %shade_1_0.1.pieces) | copy-start | bytes 12582916
  62.5 14.2 %collective-permute-start.10 = (f32[4,64,512]{2,1,0:T(8,128)}, f32[4,64,512]{2,1,0:T(8,128)S(1)}, u32[]{:S(2)}, u32[]{:S(2)}) collective-permute-start(f32[4,64,512]{2,1,0:T(8,128)} %get-tuple-element.25), channel_id=1, source_target_pairs={{0,8},{8,16},{1,9},{9,17},{2,10},{10,18},{3,11},{11,19},{4,12},{12... | collective-permute-start | bytes 1572872 | tf_op jit(solution)/shard_map/ppermute | solution.py:450
  65.7 10.9 %collective-permute-start.11 = (f32[4,64,512]{2,1,0:T(8,128)S(1)}, f32[4,64,512]{2,1,0:T(8,128)S(1)}, u32[]{:S(2)}, u32[]{:S(2)}) collective-permute-start(f32[4,64,512]{2,1,0:T(8,128)S(1)} %get-tuple-element.26), channel_id=1, source_target_pairs={{24,16},{16,8},{25,17},{17,9},{26,18},{18,10},{27,19},{19,11},{28,... | collective-permute-start | bytes 1572872 | tf_op jit(solution)/shard_map/ppermute | solution.py:451
  68.0 23.6 %collective-permute-start.5 = (f32[4,64,512]{2,1,0:T(8,128)}, f32[4,64,512]{2,1,0:T(8,128)S(1)}, u32[]{:S(2)}, u32[]{:S(2)}) collective-permute-start(f32[4,64,512]{2,1,0:T(8,128)} %get-tuple-element.21), channel_id=1, source_target_pairs={{0,8},{8,16},{1,9},{9,17},{2,10},{10,18},{3,11},{11,19},{4,12},{12... | collective-permute-start | bytes 1572872 | tf_op jit(solution)/shard_map/ppermute | solution.py:450
  73.5 18.0 %collective-permute-start.6 = (f32[4,64,512]{2,1,0:T(8,128)S(1)}, f32[4,64,512]{2,1,0:T(8,128)S(1)}, u32[]{:S(2)}, u32[]{:S(2)}) collective-permute-start(f32[4,64,512]{2,1,0:T(8,128)S(1)} %get-tuple-element.22), channel_id=1, source_target_pairs={{24,16},{16,8},{25,17},{17,9},{26,18},{18,10},{27,19},{19,11},{28,... | collective-permute-start | bytes 1572872 | tf_op jit(solution)/shard_map/ppermute | solution.py:451
  76.7 2.2 %copy-start.1 = (f32[4,2,4,64,512]{4,3,2,1,0:T(8,128)S(1)}, f32[4,2,4,64,512]{4,3,2,1,0:T(8,128)}, u32[]{:S(2)}) copy-start(f32[4,2,4,64,512]{4,3,2,1,0:T(8,128)} %shade_1_0.1.pieces) | copy-start | bytes 12582916
  80.6 21.0 %collective-permute-start.12 = (f32[4,64,512]{2,1,0:T(8,128)}, f32[4,64,512]{2,1,0:T(8,128)S(1)}, u32[]{:S(2)}, u32[]{:S(2)}) collective-permute-start(f32[4,64,512]{2,1,0:T(8,128)} %get-tuple-element.27), channel_id=1, source_target_pairs={{0,8},{8,16},{16,24},{1,9},{9,17},{17,25},{2,10},{10,18},{18,26},{... | collective-permute-start | bytes 1572872 | tf_op jit(solution)/shard_map/ppermute | solution.py:450
  90.2 18.4 %collective-permute-start.13 = (f32[4,64,512]{2,1,0:T(8,128)}, f32[4,64,512]{2,1,0:T(8,128)S(1)}, u32[]{:S(2)}, u32[]{:S(2)}) collective-permute-start(f32[4,64,512]{2,1,0:T(8,128)} %get-tuple-element.28), channel_id=1, source_target_pairs={{24,16},{16,8},{8,0},{25,17},{17,9},{9,1},{26,18},{18,10},{10,2},{... | collective-permute-start | bytes 1572872 | tf_op jit(solution)/shard_map/ppermute | solution.py:451
  92.3 20.4 %collective-permute-start.7 = (f32[4,64,512]{2,1,0:T(8,128)S(1)}, f32[4,64,512]{2,1,0:T(8,128)S(1)}, u32[]{:S(2)}, u32[]{:S(2)}) collective-permute-start(f32[4,64,512]{2,1,0:T(8,128)S(1)} %get-tuple-element.23), channel_id=1, source_target_pairs={{0,8},{8,16},{16,24},{1,9},{9,17},{17,25},{2,10},{10,18},{18,26},{... | collective-permute-start | bytes 1572872 | tf_op jit(solution)/shard_map/ppermute | solution.py:450
  98.4 21.0 %collective-permute-start.8 = (f32[4,64,512]{2,1,0:T(8,128)S(1)}, f32[4,64,512]{2,1,0:T(8,128)S(1)}, u32[]{:S(2)}, u32[]{:S(2)}) collective-permute-start(f32[4,64,512]{2,1,0:T(8,128)S(1)} %get-tuple-element.24), channel_id=1, source_target_pairs={{24,16},{16,8},{8,0},{25,17},{17,9},{9,1},{26,18},{18,10},{10,2},{... | collective-permute-start | bytes 1572872 | tf_op jit(solution)/shard_map/ppermute | solution.py:451
  108.6 2.2 %copy-start.2 = (f32[4,2,4,64,512]{4,3,2,1,0:T(8,128)S(1)}, f32[4,2,4,64,512]{4,3,2,1,0:T(8,128)}, u32[]{:S(2)}) copy-start(f32[4,2,4,64,512]{4,3,2,1,0:T(8,128)} %shade_1_0.1.pieces) | copy-start | bytes 12582916
